TPU v7x, 32 devices: a whole 2x2x4 slice. The times are simulated.
32 devices in a mesh: lat: 16 (over z, y, x), lev: 2 (over core).
Axes of the slice: x: 2, y: 2, z: 4, core: 2. Of those that a mesh axis runs over, the one named last changes fastest.
Arguments:
- grid: bfloat16 [96, 2, 48, 400], P('lat', None, 'lev'), may hold values from -6 to 6
- point_counts: int32 [96], P('lat'), may hold values from 16 to 400, as said below
- waves: int32 [96], replicated, may hold values from 0 to 95, each once
- legendre: bfloat16 [96, 96, 96], P('lat'), may hold values from -0.625 to 0.625
- weights: float32 [96], P('lat'), may hold values from 0.5 to 2
- stiffness: float32 [48], replicated, may hold values from 1e-06 to 0.0001
Outputs:
- grid_out: bfloat16 [96, 2, 48, 400], P('lat', None, 'lev')
Inputs may be any that keep to these rules, and one draw needn't show every extreme that they name: point_counts[j] is 4 j + 16 or 4 j + 20 (j counted from 0 at the pole), and the last pair has exactly 400 points. `waves`: each wavenumber from 0 to 95 appears once.
All inputs are finite; a program needn't handle non-finite values.
Results may differ from a plain program's by a relative error of at most 0.015.
Values may be sent and summed in bfloat16 or wider, within the bound.
No kernel may reach another device: no remote copies, remote signals or barrier semaphores. Data moves between devices by JAX's collectives and lax.ppermute only.
A program may use at most 128 MiB of HBM per device.

v0:
```python
import math

import jax
import jax.numpy as jnp
from jax import lax
from jax.sharding import PartitionSpec as P

TWO_PI = 2.0 * math.pi
FINE_STEPS = 32


def fourier_tables(count, wavenumbers, quarter_max):
    quarter = count // 4
    step_angle = TWO_PI / quarter.astype(jnp.float32)
    coarse_count = (quarter_max + FINE_STEPS - 1) // FINE_STEPS
    coarse_pos = FINE_STEPS * jnp.arange(coarse_count, dtype=jnp.int32)
    fine_pos = jnp.arange(FINE_STEPS, dtype=jnp.int32)
    coarse_angle = (coarse_pos[:, None] * wavenumbers[None, :] % quarter).astype(
        jnp.float32
    ) * step_angle
    fine_angle = (fine_pos[:, None] * wavenumbers[None, :] % quarter).astype(
        jnp.float32
    ) * step_angle
    coarse_cos = jnp.cos(coarse_angle)[:, None, :]
    coarse_sin = jnp.sin(coarse_angle)[:, None, :]
    fine_cos = jnp.cos(fine_angle)[None, :, :]
    fine_sin = jnp.sin(fine_angle)[None, :, :]
    full_cos = (coarse_cos * fine_cos - coarse_sin * fine_sin).reshape(
        coarse_count * FINE_STEPS, -1
    )[:quarter_max]
    full_sin = (coarse_sin * fine_cos + coarse_cos * fine_sin).reshape(
        coarse_count * FINE_STEPS, -1
    )[:quarter_max]
    positions = jnp.arange(quarter_max, dtype=jnp.int32)
    inside = (positions < quarter)[:, None]
    cosine = jnp.where(inside, full_cos, 0.0)
    sine = jnp.where(inside, full_sin, 0.0)
    matrix = jnp.concatenate([cosine, sine], axis=1).astype(jnp.bfloat16)
    offsets = jnp.arange(4, dtype=jnp.int32)
    twist = offsets[:, None] * wavenumbers[None, :] % count
    theta = twist.astype(jnp.float32) * (TWO_PI / count.astype(jnp.float32))
    return (matrix, jnp.cos(theta), jnp.sin(theta))


def helmholtz(spectra, wavenumbers, offsets, stiffness_local, width):
    full_shape = spectra.shape
    quartered = spectra.reshape(full_shape[:-2] + (full_shape[-2] // 4, 2, 2, full_shape[-1]))
    parity = (1 - 2 * (offsets % 2)).astype(jnp.float32)
    combined = quartered[..., 0, :] + parity * quartered[..., 1, :]
    degrees = (wavenumbers + offsets).astype(jnp.float32)
    inside_band = offsets < width - wavenumbers
    factor = 1.0 / (
        1.0 + stiffness_local[:, None] * degrees[..., None, :] * (degrees[..., None, :] + 1.0)
    )
    damping = jnp.where(inside_band[..., None, :], factor, 0.0)
    scaled = (combined * damping[..., :, None, :]).astype(jnp.bfloat16)
    flipped = scaled * parity.astype(jnp.bfloat16)
    return jnp.stack([scaled, flipped], axis=-2).reshape(full_shape)


def spectral(received, wavenumbers, basis, stiffness_local):
    width = basis.shape[2]
    spectra = jnp.einsum("jcr,cjl->crl", received, basis, preferred_element_type=jnp.float32)
    offsets = jnp.arange(width, dtype=jnp.int32)
    operand = helmholtz(spectra, wavenumbers[:, None], offsets, stiffness_local, width)
    returned = jnp.einsum("crl,cjl->jcr", operand, basis, preferred_element_type=jnp.float32)
    return returned.astype(jnp.bfloat16)


def on_device(grid, point_counts, waves, legendre, weights, stiffness):
    pairs, _, fields, points = grid.shape
    quarter_max = points // 4
    width = waves.shape[0]
    held_slots = legendre.shape[0]
    lat_index = lax.axis_index("lat")
    lev_index = lax.axis_index("lev")

    def analyse(pieces):
        latitude, count, weight = pieces
        matrix, twist_cos, twist_sin = fourier_tables(count, waves, quarter_max)
        values = latitude.reshape(2, fields, quarter_max, 4)
        partial_value = jnp.einsum(
            "hfab,at->hfbt", values, matrix, preferred_element_type=jnp.float32
        )
        cos_part = partial_value[..., :width]
        sin_part = partial_value[..., width:]
        real = jnp.sum(twist_cos * cos_part - twist_sin * sin_part, axis=2)
        imag = -jnp.sum(twist_sin * cos_part + twist_cos * sin_part, axis=2)
        factor = jnp.where(2 * waves < count, weight / count.astype(jnp.float32), 0.0)
        stacked = jnp.stack([real * factor, imag * factor], axis=0)
        packed = jnp.transpose(stacked, (3, 2, 0, 1)).reshape(width, 4 * fields)
        return (packed.astype(jnp.bfloat16), matrix, twist_cos, twist_sin)

    coefficients, matrices, twist_cos, twist_sin = lax.map(analyse, (grid, point_counts, weights))
    received = lax.all_to_all(coefficients, "lat", split_axis=1, concat_axis=0, tiled=True)
    owned = lax.dynamic_slice_in_dim(waves, lat_index * held_slots, held_slots)
    own_stiffness = lax.dynamic_slice_in_dim(stiffness, lev_index * fields, fields)
    synthesised = spectral(received, owned, legendre, own_stiffness)
    returned = lax.all_to_all(synthesised, "lat", split_axis=0, concat_axis=1, tiled=True)

    def synthesise(pieces):
        packed, matrix, turn_cos, turn_sin, count = pieces
        values = packed.astype(jnp.float32).reshape(width, fields, 2, 2)
        real = values[:, :, 0, :]
        imag = values[:, :, 1, :]
        factor = jnp.where(2 * waves < count, jnp.where(waves == 0, 1.0, 2.0), 0.0)[:, None, None]
        cosines = turn_cos[:, :, None, None]
        sines = turn_sin[:, :, None, None]
        turned_real = factor * (real * cosines - imag * sines)
        turned_imag = factor * (real * sines + imag * cosines)
        operand = jnp.concatenate([turned_real, -turned_imag], axis=1)
        upper = operand.astype(jnp.bfloat16)
        lower = (operand - upper.astype(jnp.float32)).astype(jnp.bfloat16)
        result = jnp.einsum("bmfh,am->hfab", upper, matrix, preferred_element_type=jnp.float32)
        result = result + jnp.einsum(
            "bmfh,am->hfab", lower, matrix, preferred_element_type=jnp.float32
        )
        return result.reshape(2, fields, points).astype(jnp.bfloat16)

    return lax.map(synthesise, (returned, matrices, twist_cos, twist_sin, point_counts))


def solution(mesh):
    in_specs = (P("lat", None, "lev", None), P("lat"), P(), P("lat", None, None), P("lat"), P())
    out_specs = P("lat", None, "lev", None)
    return jax.shard_map(
        on_device, mesh=mesh, in_specs=in_specs, out_specs=out_specs, check_vma=False
    )
```

profile of v0, /device:TPU:0, one launch (start us, length us, event | category | flops | bytes accessed | tf_op | source)
XLA Modules:
  0.0 100.6 jit_solution(9834222721202018338)
XLA Ops:
  0.0 0.7 copy-done.1
  0.7 53.4 %while.28 = (s32[]{:T(128)}, bf16[6,96,96]{1,2,0:T(8,128)(2,1)S(1)}, bf16[6,100,192]{1,2,0:T(8,128)(2,1)S(1)}, f32[6,4,96]{2,1,0:T(4,128)S(1)}, f32[6,4,96]{2,1,...) while((s32[]{:T(128)}, ...), condition=%wide.region_3.4_spmd, body=%wide.region_0.3_spmd.sunk | while | flops 7857060 | bytes 1186901 | solution.py:94
  0.7 0.6 dynamic_slice.69
  6.2 0.8 constant_dynamic-slice_fusion.4
  7.5 0.6 dynamic_slice.70
  8.8 0.6 compare_select_fusion.5
  9.6 0.6 dynamic_slice.69
  15.1 0.8 constant_dynamic-slice_fusion.4
  16.5 0.6 dynamic_slice.70
  17.7 0.6 compare_select_fusion.5
  18.5 0.6 dynamic_slice.69
  24.0 0.8 constant_dynamic-slice_fusion.4
  25.4 0.6 dynamic_slice.70
  26.6 0.6 compare_select_fusion.5
  27.4 0.6 dynamic_slice.69
  32.9 0.8 constant_dynamic-slice_fusion.4
  34.3 0.6 dynamic_slice.70
  35.5 0.6 compare_select_fusion.5
  36.3 0.6 dynamic_slice.69
  41.9 0.8 constant_dynamic-slice_fusion.4
  43.2 0.6 dynamic_slice.70
  44.4 0.6 compare_select_fusion.5
  45.2 0.6 dynamic_slice.69
  50.8 0.8 constant_dynamic-slice_fusion.4
  52.1 0.6 dynamic_slice.70
  53.3 0.6 compare_select_fusion.5
  54.1 0.8 copy.35
  55.0 8.4 %all-to-all-start = ((bf16[6,96,96]{2,0,1:T(8,128)(2,1)}), bf16[6,96,96]{2,0,1:T(8,128)(2,1)S(1)}, u32[]{:S(2)}, u32[]{:S(2)}) async-start(bf16[6,96,96]{2,0,1:T(8,128)(2,1)} %copy.35), calls=%async_computation | async-start | bytes 393216 | tf_op jit(solution)/shard_map/all_to_all | solution.py:95
  63.7 0.7 copy-done.4
  64.5 7.5 %all-to-all-done = bf16[6,96,96]{2,0,1:T(8,128)(2,1)S(1)} async-done(((bf16[6,96,96]{2,0,1:T(8,128)(2,1)}), bf16[6,96,96]{2,0,1:T(8,128)(2,1)S(1)}, u32[]{:S(2)}, u32[]{:S(2)}) %all-to-all-start) | async-done | bytes 110624 | tf_op jit(solution)/shard_map/all_to_all | solution.py:95
  72.7 0.4 pad_maximum_fusion.1
  73.3 0.8 copy.39
  74.1 3.5 %all-to-all-start.1 = ((bf16[96,6,96]{2,1,0:T(8,128)(2,1)}), bf16[96,6,96]{2,1,0:T(8,128)(2,1)S(1)}, u32[]{:S(2)}, u32[]{:S(2)}) async-start(bf16[96,6,96]{2,1,0:T(8,128)(2,1)} %copy.39), calls=%async_computation.1 | async-start | bytes 393216 | tf_op jit(solution)/shard_map/all_to_all | solution.py:99
  77.7 8.0 %all-to-all-done.1 = bf16[96,6,96]{2,1,0:T(8,128)(2,1)S(1)} async-done(((bf16[96,6,96]{2,1,0:T(8,128)(2,1)}), bf16[96,6,96]{2,1,0:T(8,128)(2,1)S(1)}, u32[]{:S(2)}, u32[]{:S(2)}) %all-to-all-start.1) | async-done | bytes 110624 | tf_op jit(solution)/shard_map/all_to_all | solution.py:99
  85.8 14.0 %while.29 = (s32[]{:T(128)}, bf16[6,2,24,400]{3,2,1,0:T(8,128)(2,1)S(1)}, bf16[6,100,192]{1,2,0:T(8,128)(2,1)S(1)}, s32[96]{0:T(128)S(1)}, s32[6]{0:T(128)S(1)},...) while((s32[]{:T(128)}, ...), condition=%wide.region_5.6_spmd, body=%wide.region_4.5_spmd.sunk | while | flops 15291362 | bytes 1428225 | solution.py:120
  86.1 0.6 dynamic_slice.75
  86.7 0.6 compare_select_fusion.6
  88.4 0.6 dynamic_slice.75
  89.0 0.6 compare_select_fusion.6
  90.8 0.6 dynamic_slice.75
  91.4 0.6 compare_select_fusion.6
  93.1 0.6 dynamic_slice.75
  93.7 0.6 compare_select_fusion.6
  95.4 0.6 dynamic_slice.75
  96.0 0.6 compare_select_fusion.6
  97.8 0.6 dynamic_slice.75
  98.4 0.6 compare_select_fusion.6
  99.9 0.7 copy-done.2
  (220 shorter events, 16.9 us)
Async XLA Ops:
  0.0 72.1 %copy-start = (bf16[6,96,96]{2,1,0:T(8,128)(2,1)S(1)}, bf16[6,96,96]{2,1,0:T(8,128)(2,1)}, u32[]{:S(2)}) copy-start(bf16[6,96,96]{2,1,0:T(8,128)(2,1)} %param.13) | copy-start | bytes 331780
  0.0 0.7 copy-start.1
  0.0 0.7 copy-start.3
  0.0 0.7 copy-start.5
  55.0 17.0 %all-to-all-start = ((bf16[6,96,96]{2,0,1:T(8,128)(2,1)}), bf16[6,96,96]{2,0,1:T(8,128)(2,1)S(1)}, u32[]{:S(2)}, u32[]{:S(2)}) async-start(bf16[6,96,96]{2,0,1:T(8,128)(2,1)} %copy.35), calls=%async_computation | async-start | bytes 393216 | tf_op jit(solution)/shard_map/all_to_all | solution.py:95
  63.7 0.7 copy-start.4
  74.1 11.6 %all-to-all-start.1 = ((bf16[96,6,96]{2,1,0:T(8,128)(2,1)}), bf16[96,6,96]{2,1,0:T(8,128)(2,1)S(1)}, u32[]{:S(2)}, u32[]{:S(2)}) async-start(bf16[96,6,96]{2,1,0:T(8,128)(2,1)} %copy.39), calls=%async_computation.1 | async-start | bytes 393216 | tf_op jit(solution)/shard_map/all_to_all | solution.py:99
  99.9 0.7 copy-start.2
where the time goes:
time: 102 us; the launch traced here: 101 us
  loops' own time  29.3 us (29%)
  local copies, waits for them, and re-layouts  24.9 us (24%)
  waiting for transfers between devices  15.5 us (15%)
  other arithmetic  14.2 us (14%)
  starting transfers between devices  11.9 us (12%)
  matrix products  4.6 us (5%)
    another operation x1, loops' own time, on_device(): lax.map(analyse, (grid, point_counts, weights))  28.8 us
    dynamic_slice x30, local copies, waits for them, and re-layouts, on_device(): lax.map(analyse, (grid, point_counts, weights))  16.5 us
    all_to_all x1, starting transfers between devices, on_device(): lax.all_to_all(coefficients, 'lat', split_axis=1, concat_axis=0, tiled=True)  8.35 us
    all_to_all x1, waiting for transfers between devices, on_device(): lax.all_to_all(synthesised, 'lat', split_axis=0, concat_axis=1, tiled=True)  8.03 us
    all_to_all x1, waiting for transfers between devices, on_device(): lax.all_to_all(coefficients, 'lat', split_axis=1, concat_axis=0, tiled=True)  7.5 us
    select_n x6, other arithmetic, synthesise(): jnp.where(2 * waves < count, jnp.where(waves == 0, 1.0, 2.0), 0.0)  3.89 us
    all_to_all x1, starting transfers between devices, on_device(): lax.all_to_all(synthesised, 'lat', split_axis=0, concat_axis=1, tiled=True)  3.52 us
    select_n x6, other arithmetic, analyse(): jnp.where(2 * waves < count, weight / count.astype(jnp.float32), 0.0)  3.37 us
  transfers between devices with their start and end apart: 2, of which 2 were waited for; matrix products, arithmetic and copies ran while one was open for 0% of the time, Pallas kernels for 0%

commit v1 on v0

--- a/solution.py
+++ b/solution.py
@@ -1,12 +1,226 @@
+import functools
 import math
 
 import jax
 import jax.numpy as jnp
 from jax import lax
+from jax.experimental import pallas as pl
+from jax.experimental.pallas import tpu as pltpu
 from jax.sharding import PartitionSpec as P
 
 TWO_PI = 2.0 * math.pi
 FINE_STEPS = 32
+LANES = 128
+ROWS = 8
+TABLE_BUDGET = 16 << 20
+
+COS_TURN = (
+    0.9999999998781397, -19.739208740145937, 64.9393888386778, -85.45665201444898,
+    60.24205245141228, -26.404165331517056, 7.79855301354287, -1.4511773940976733,
+)
+SIN_TURN = (
+    6.2831853022485955, -41.341700317335295, 81.60512671223316, -76.70292598092092,
+    42.02516399730493, -14.896874459689428, 3.233831551278599,
+)
+
+
+def polynomial(coefficients, u):
+    total = coefficients[-1] * u + coefficients[-2]
+    for value in coefficients[-3::-1]:
+        total = total * u + value
+    return total
+
+
+def cos_minus_sin(steps, count, inverse):
+    reduced = steps - jnp.floor(steps * inverse + 0.5) * count
+    turn = reduced * inverse
+    square = turn * turn
+    return polynomial(COS_TURN, square), -turn * polynomial(SIN_TURN, square)
+
+
+def wave_column(waves_ref, held, slots):
+    width = waves_ref.shape[1]
+    row = lax.broadcasted_iota(jnp.int32, (slots, width), 0)
+    lane = lax.broadcasted_iota(jnp.int32, (slots, width), 1)
+    place = row & (ROWS - 1)
+    chosen = ((row >> 3) * held + place == lane) & (place < held)
+    waves = jnp.broadcast_to(waves_ref[...].astype(jnp.float32), (slots, width))
+    column = jnp.sum(jnp.where(chosen, waves, 0.0), axis=1, keepdims=True)
+    filled = (lax.broadcasted_iota(jnp.int32, (slots, 1), 0) & (ROWS - 1)) < held
+    return column, filled
+
+
+def analysis_kernel(held, counts, weights, waves_ref, grid_hbm, coef_ref, table_ref, values, arrived):
+    owners, pairs, _, _ = coef_ref.shape
+    slots = owners * ROWS
+    points = grid_hbm.shape[1]
+    rows = grid_hbm.shape[0] // pairs
+    fetch = pltpu.make_async_copy(grid_hbm, values, arrived)
+    fetch.start()
+    wave, filled = wave_column(waves_ref, held, slots)
+    lane = lax.broadcasted_iota(jnp.int32, (1, LANES), 1)
+    lane_count = jnp.ones((1, LANES), jnp.float32)
+    for j in range(pairs):
+        lane_count = jnp.where(lane == j, counts[j].astype(jnp.float32), lane_count)
+    lane_inverse = 1.0 / lane_count
+    turn_cos, turn_sin = cos_minus_sin(
+        jnp.broadcast_to(wave * float(LANES), (slots, LANES)), lane_count, lane_inverse
+    )
+    steps = wave * lane.astype(jnp.float32)
+    blocks = table_ref.shape[2] // LANES
+    for j in range(pairs):
+        count = jnp.full((1, LANES), counts[j].astype(jnp.float32))
+        inverse = 1.0 / count
+        cosine, sine = cos_minus_sin(steps, count, inverse)
+        kept = filled & (2.0 * wave < count[:, :1])
+        cosine = jnp.where(kept, cosine, 0.0)
+        sine = jnp.where(kept, sine, 0.0)
+        block_cos = turn_cos[:, j : j + 1]
+        block_sin = turn_sin[:, j : j + 1]
+        for block in range(blocks):
+            if block > 0:
+                cosine, sine = (
+                    cosine * block_cos - sine * block_sin,
+                    sine * block_cos + cosine * block_sin,
+                )
+            at = pl.ds(block * LANES, LANES)
+            table_ref[j, :slots, at] = cosine.astype(jnp.bfloat16)
+            table_ref[j, slots:, at] = sine.astype(jnp.bfloat16)
+    fetch.wait()
+    position = lax.broadcasted_iota(jnp.int32, (1, points), 1)
+    for j in range(pairs):
+        inside = jnp.where(position < counts[j], 1.0, 0.0).astype(jnp.bfloat16)
+        latitude = values[j * rows : (j + 1) * rows, :] * inside
+        product = lax.dot_general(
+            table_ref[j, :, :points],
+            latitude,
+            (((1,), (1,)), ((), ())),
+            preferred_element_type=jnp.float32,
+        )
+        scale = jnp.full((1, 1), weights[j]) / jnp.full((1, 1), counts[j].astype(jnp.float32))
+        product = product * scale
+        packed = jnp.concatenate(
+            [
+                product[:slots],
+                product[slots:],
+                jnp.zeros((slots, LANES - 2 * rows), jnp.float32),
+            ],
+            axis=1,
+        )
+        coef_ref[:, j] = packed.reshape(owners, ROWS, LANES).astype(jnp.bfloat16)
+
+
+def legendre_kernel(held, fields, waves, stiffness_ref, basis_ref, recv_ref, send_ref, fan_in, fan_out):
+    owners, pairs, _, _ = recv_ref.shape
+    latitudes = owners * pairs
+    width = basis_ref.shape[2]
+    first = lax.axis_index("lat") * held
+    fan_in[...] = recv_ref[...].astype(jnp.float32).reshape(latitudes * ROWS, LANES)
+    lane = lax.broadcasted_iota(jnp.int32, (1, LANES), 1)
+    own = pltpu.roll(stiffness_ref[...], (LANES - lax.axis_index("lev") * fields) % LANES, 1)
+    own = jnp.where(lane < fields, own, 0.0)
+    stiffness = own
+    for copy in range(1, 4):
+        stiffness = stiffness + pltpu.roll(own, copy * fields, 1)
+    south = ((lane >= fields) & (lane < 2 * fields)) | (lane >= 3 * fields)
+    offset = lax.broadcasted_iota(jnp.int32, (width, 1), 0)
+    parity = jnp.where((offset & 1) == 0, 1.0, -1.0)
+    for c in range(held):
+        wave = waves[first + c]
+        degree = (offset + wave).astype(jnp.float32)
+        factor = 1.0 / (1.0 + stiffness * degree * (degree + 1.0))
+        damping = jnp.where(offset < width - wave, factor, 0.0)
+        block = fan_in[pl.ds(c, latitudes, stride=ROWS), :].astype(jnp.bfloat16)
+        basis = basis_ref[c]
+        spectra = lax.dot_general(
+            basis, block, (((0,), (0,)), ((), ())), preferred_element_type=jnp.float32
+        )
+        other = jnp.where(
+            south, pltpu.roll(spectra, fields, 1), pltpu.roll(spectra, LANES - fields, 1)
+        )
+        scaled = ((spectra + parity * other) * damping).astype(jnp.bfloat16)
+        returned = jnp.dot(basis, scaled, preferred_element_type=jnp.float32)
+        returned = returned * jnp.where(wave == 0, 1.0, 2.0)
+        fan_out[pl.ds(c, latitudes, stride=ROWS), :] = returned
+    for c in range(held, ROWS):
+        fan_out[pl.ds(c, latitudes, stride=ROWS), :] = jnp.zeros((latitudes, LANES), jnp.float32)
+    send_ref[...] = fan_out[...].reshape(owners, pairs, ROWS, LANES).astype(jnp.bfloat16)
+
+
+def synthesis_kernel(counts, recv_ref, table_ref, grid_hbm, values, left):
+    owners, pairs, _, _ = recv_ref.shape
+    slots = owners * ROWS
+    points = grid_hbm.shape[1]
+    rows = grid_hbm.shape[0] // pairs
+    position = lax.broadcasted_iota(jnp.int32, (1, points), 1)
+    copies = []
+    for j in range(pairs):
+        block = recv_ref[:, j].astype(jnp.float32).reshape(slots, LANES)
+        operand = jnp.concatenate([block[:, :rows], block[:, rows : 2 * rows]], axis=0)
+        product = lax.dot_general(
+            operand.astype(jnp.bfloat16),
+            table_ref[j],
+            (((0,), (0,)), ((), ())),
+            preferred_element_type=jnp.float32,
+        )
+        kept = jnp.where(position < counts[j], product[:, :points], 0.0)
+        at = pl.ds(j * rows, rows)
+        values[at, :] = kept.astype(jnp.bfloat16)
+        copies.append(pltpu.make_async_copy(values.at[at, :], grid_hbm.at[at, :], left.at[j]))
+        copies[-1].start()
+    for copy in copies:
+        copy.wait()
+
+
+def on_device(grid, point_counts, waves, legendre, weights, stiffness):
+    pairs, _, fields, points = grid.shape
+    held = legendre.shape[0]
+    width = waves.shape[0]
+    owners = width // held
+    slots = owners * ROWS
+    rows = 2 * fields
+    padded = -(-points // LANES) * LANES
+    smem = pl.BlockSpec(memory_space=pltpu.SMEM)
+    vmem = pl.BlockSpec(memory_space=pltpu.VMEM)
+    anywhere = pl.BlockSpec(memory_space=pl.ANY)
+    exchanged = jax.ShapeDtypeStruct((owners, pairs, ROWS, LANES), jnp.bfloat16)
+    coefficients, tables = pl.pallas_call(
+        functools.partial(analysis_kernel, held),
+        out_shape=(exchanged, jax.ShapeDtypeStruct((pairs, 2 * slots, padded), jnp.bfloat16)),
+        in_specs=[smem, smem, vmem, anywhere],
+        out_specs=(vmem, vmem),
+        scratch_shapes=[
+            pltpu.VMEM((pairs * rows, points), jnp.bfloat16),
+            pltpu.SemaphoreType.DMA,
+        ],
+        name="analysis",
+    )(point_counts, weights, waves.reshape(1, width), grid.reshape(pairs * rows, points))
+    received = lax.all_to_all(coefficients, "lat", split_axis=0, concat_axis=0, tiled=True)
+    lane_stiffness = jnp.pad(stiffness, (0, LANES - stiffness.shape[0])).reshape(1, LANES)
+    synthesised = pl.pallas_call(
+        functools.partial(legendre_kernel, held, fields),
+        out_shape=exchanged,
+        in_specs=[smem, vmem, vmem, vmem],
+        out_specs=vmem,
+        scratch_shapes=[
+            pltpu.VMEM((owners * pairs * ROWS, LANES), jnp.float32),
+            pltpu.VMEM((owners * pairs * ROWS, LANES), jnp.float32),
+        ],
+        name="legendre",
+    )(waves, lane_stiffness, legendre, received)
+    returned = lax.all_to_all(synthesised, "lat", split_axis=0, concat_axis=0, tiled=True)
+    result = pl.pallas_call(
+        synthesis_kernel,
+        out_shape=jax.ShapeDtypeStruct((pairs * rows, points), jnp.bfloat16),
+        in_specs=[smem, vmem, vmem],
+        out_specs=anywhere,
+        scratch_shapes=[
+            pltpu.VMEM((pairs * rows, points), jnp.bfloat16),
+            pltpu.SemaphoreType.DMA((pairs,)),
+        ],
+        name="synthesis",
+    )(point_counts, returned, tables)
+    return result.reshape(grid.shape)
 
 
 def fourier_tables(count, wavenumbers, quarter_max):
@@ -67,7 +281,7 @@
     return returned.astype(jnp.bfloat16)
 
 
-def on_device(grid, point_counts, waves, legendre, weights, stiffness):
+def on_device_blocked(grid, point_counts, waves, legendre, weights, stiffness):
     pairs, _, fields, points = grid.shape
     quarter_max = points // 4
     width = waves.shape[0]
@@ -120,9 +334,28 @@
     return lax.map(synthesise, (returned, matrices, twist_cos, twist_sin, point_counts))
 
 
+def fits_on_chip(mesh, grid, legendre, stiffness):
+    owners, levels = mesh.shape["lat"], mesh.shape["lev"]
+    pairs, fields = grid.shape[0] // owners, grid.shape[2] // levels
+    held = legendre.shape[0] // owners
+    table_bytes = 4 * pairs * owners * ROWS * grid.shape[3]
+    return (
+        table_bytes <= TABLE_BUDGET
+        and held <= ROWS
+        and 4 * fields <= LANES
+        and fields % ROWS == 0
+        and stiffness.shape[0] <= LANES
+    )
+
+
 def solution(mesh):
     in_specs = (P("lat", None, "lev", None), P("lat"), P(), P("lat", None, None), P("lat"), P())
     out_specs = P("lat", None, "lev", None)
-    return jax.shard_map(
-        on_device, mesh=mesh, in_specs=in_specs, out_specs=out_specs, check_vma=False
-    )
+
+    def program(grid, point_counts, waves, legendre, weights, stiffness):
+        body = on_device if fits_on_chip(mesh, grid, legendre, stiffness) else on_device_blocked
+        return jax.shard_map(
+            body, mesh=mesh, in_specs=in_specs, out_specs=out_specs, check_vma=False
+        )(grid, point_counts, waves, legendre, weights, stiffness)
+
+    return program

time: 102 us -> 38.4 us (0.38); the launches traced: 101 us -> 38 us
  loops' own time: 29.3 us -> 0 us
  local copies, waits for them, and re-layouts: 24.9 us -> 1.85 us
  other arithmetic: 14.2 us -> 0 us
  blocking collectives: 0 us -> 12.3 us
  Pallas kernels: 0 us -> 8.1 us
  waiting for transfers between devices: 15.5 us -> 7.46 us
  matrix products: 4.6 us -> 0 us
  starting transfers between devices: 11.9 us -> 8.35 us
    another operation x2 -> x0, loops' own time: 29.3 us -> none  [the longest x1 28.8 us: on_device(): lax.map(analyse, (grid, point_counts, weights))]
    dynamic_slice x43 -> x0, local copies, waits for them, and re-layouts: 17.2 us -> none  [the longest x30 16.5 us: on_device(): lax.map(analyse, (grid, point_counts, weights))]
    all_to_all x0 -> x1, blocking collectives: none -> 12.3 us  [on_device(): lax.all_to_all(synthesised, 'lat', split_axis=0, concat_axis=0, tiled=True)]
    pallas_call x0 -> x3, Pallas kernels: none -> 8.1 us  [the longest x1 3.09 us: on_device(): pl.pallas_call(functools.partial(analysis_kernel, held), out_shape=(excha...]
    all_to_all x2 -> x1, waiting for transfers between devices: 15.5 us -> 7.46 us  [on_device(): lax.all_to_all(coefficients, 'lat', split_axis=0, concat_axis=0, tiled=True)]
    select_n x13 -> x0, other arithmetic: 7.35 us -> none  [the longest x6 3.89 us: synthesise(): jnp.where(2 * waves < count, jnp.where(waves == 0, 1.0, 2.0), 0.0)]
    dot_general x20 -> x0, matrix products: 4.6 us -> none  [the longest x6 1.45 us: synthesise(): jnp.einsum('bmfh,am->hfab', lower, matrix, preferred_element_type=jnp.flo...]
    all_to_all x2 -> x1, starting transfers between devices: 11.9 us -> 8.35 us  [on_device(): lax.all_to_all(coefficients, 'lat', split_axis=0, concat_axis=0, tiled=True)]
  transfers between devices with their start and end apart: 2 -> 1, of which waited for: 2 -> 1; matrix products, arithmetic and copies ran while one was open for 0% -> 3% of each run, Pallas kernels for 0% -> 0%
where the time goes in v1:
time: 38.4 us; the launch traced here: 38 us
  blocking collectives  12.3 us (32%)
  starting transfers between devices  8.35 us (22%)
  Pallas kernels  8.1 us (21%)
  waiting for transfers between devices  7.46 us (19%)
  local copies, waits for them, and re-layouts  1.85 us (5%)
    all_to_all x1, blocking collectives, on_device(): lax.all_to_all(synthesised, 'lat', split_axis=0, concat_axis=0, tiled=True)  12.3 us
    all_to_all x1, starting transfers between devices, on_device(): lax.all_to_all(coefficients, 'lat', split_axis=0, concat_axis=0, tiled=True)  8.35 us
    all_to_all x1, waiting for transfers between devices, on_device(): lax.all_to_all(coefficients, 'lat', split_axis=0, concat_axis=0, tiled=True)  7.46 us
    pallas_call x1, Pallas kernels, on_device(): pl.pallas_call(functools.partial(analysis_kernel, held), out_shape=(excha...  3.09 us
    pallas_call x1, Pallas kernels, on_device(): pl.pallas_call(synthesis_kernel, out_shape=jax.ShapeDtypeStruct((pairs *...  2.77 us
    pallas_call x1, Pallas kernels, on_device(): pl.pallas_call(functools.partial(legendre_kernel, held, fields), out_shap...  2.24 us
    reshape x1, local copies, waits for them, and re-layouts, on_device(): jnp.pad(stiffness, (0, LANES - stiffness.shape[0])).reshape(1, LANES)  1.18 us
  transfers between devices with their start and end apart: 1, of which 1 were waited for; matrix products, arithmetic and copies ran while one was open for 3% of the time, Pallas kernels for 0%

profile of v1, /device:TPU:0, one launch (start us, length us, event | category | flops | bytes accessed | tf_op | source)
XLA Modules:
  0.0 38.0 jit_solution(9266779954276798764)
XLA Ops:
  0.0 3.1 %analysis.1 = (bf16[16,6,8,128]{3,2,1,0:T(8,128)(2,1)}, bf16[6,256,512]{2,1,0:T(8,128)(2,1)}) custom-call(s32[6]{0:T(128)} %counts.3, f32[6]{0:T(128)} %weights.1, s32[1,96]{1,0:T(1,128)} %bitcast.6, bf16[288,400]{1,0:T(8,128)(2,1)} %bitcast.5), custom_call_target="tpu_custom_call" | custom-call | tf_op jit(solution)/shard_map/analysis/pallas_call | solution.py:187
  3.1 8.4 %all-to-all-start = ((bf16[16,6,8,128]{3,2,1,0:T(8,128)(2,1)}), bf16[16,6,8,128]{3,2,1,0:T(8,128)(2,1)S(1)}, u32[]{:S(2)}, u32[]{:S(2)}) async-start(bf16[16,6,8,128]{3,2,1,0:T(8,128)(2,1)} %get-tuple-element.7), calls=%async_computation | async-start | bytes 393216 | tf_op jit(solution)/shard_map/all_to_all | solution.py:198
  11.5 1.2 %pad_bitcast_fusion.stiffness_ref = f32[1,128]{1,0:T(1,128)} fusion(f32[48]{0:T(128)} %param.11), kind=kLoop, calls=%fused_computation | loop fusion | bytes 704 | tf_op jit(solution)/shard_map/reshape | solution.py:199
  12.6 7.5 %all-to-all-done.recv_ref = bf16[16,6,8,128]{3,2,1,0:T(8,128)(2,1)S(1)} async-done(((bf16[16,6,8,128]{3,2,1,0:T(8,128)(2,1)}), bf16[16,6,8,128]{3,2,1,0:T(8,128)(2,1)S(1)}, u32[]{:S(2)}, u32[]{:S(2)}) %all-to-all-start) | async-done | bytes 196640 | tf_op jit(solution)/shard_map/all_to_all | solution.py:198
  20.1 0.0 copy-start
  20.1 0.7 %copy-done = bf16[16,6,8,128]{3,2,1,0:T(8,128)(2,1)} copy-done((bf16[16,6,8,128]{3,2,1,0:T(8,128)(2,1)}, bf16[16,6,8,128]{3,2,1,0:T(8,128)(2,1)S(1)}, u32[]{:S(2)}) %copy-start) | copy-done | bytes 196632
  20.8 2.2 %legendre.1 = bf16[16,6,8,128]{3,2,1,0:T(8,128)(2,1)} custom-call(s32[96]{0:T(128)} %waves.1, f32[1,128]{1,0:T(1,128)} %pad_bitcast_fusion.stiffness_ref, bf16[6,96,96]{2,1,0:T(8,128)(2,1)} %basis_ref.1, bf16[16,6,8,128]{3,2,1,0:T(8,128)(2,1)} %copy-done), custom_call_target="tpu_custom_call" | custom-call | tf_op jit(solution)/shard_map/legendre/pallas_call | solution.py:200
  23.0 12.3 %all_to_all.10.recv_ref = bf16[16,6,8,128]{3,2,1,0:T(8,128)(2,1)} all-to-all(bf16[16,6,8,128]{3,2,1,0:T(8,128)(2,1)} %legendre.1), channel_id=1, replica_groups=mesh['lat'=16,'lev'=2] {'lat'}, dimensions={0} | all-to-all | bytes 393216 | tf_op jit(solution)/shard_map/all_to_all | solution.py:211
  35.3 2.8 %synthesis.1 = bf16[288,400]{1,0:T(8,128)(2,1)} custom-call(s32[6]{0:T(128)} %counts.3, bf16[16,6,8,128]{3,2,1,0:T(8,128)(2,1)} %all_to_all.10.recv_ref, bf16[6,256,512]{2,1,0:T(8,128)(2,1)} %get-tuple-element.8.table_ref), custom_call_target="tpu_custom_call" | custom-call | tf_op jit(solution)/shard_map/synthesis/pallas_call | solution.py:212
Async XLA Ops:
  3.1 17.0 %all-to-all-start = ((bf16[16,6,8,128]{3,2,1,0:T(8,128)(2,1)}), bf16[16,6,8,128]{3,2,1,0:T(8,128)(2,1)S(1)}, u32[]{:S(2)}, u32[]{:S(2)}) async-start(bf16[16,6,8,128]{3,2,1,0:T(8,128)(2,1)} %get-tuple-element.7), calls=%async_computation | async-start | bytes 393216 | tf_op jit(solution)/shard_map/all_to_all | solution.py:198
  20.1 0.7 %copy-start = (bf16[16,6,8,128]{3,2,1,0:T(8,128)(2,1)}, bf16[16,6,8,128]{3,2,1,0:T(8,128)(2,1)S(1)}, u32[]{:S(2)}) copy-start(bf16[16,6,8,128]{3,2,1,0:T(8,128)(2,1)S(1)} %all-to-all-done.recv_ref) | copy-start | bytes 589828

commit v2 on v1

--- a/solution.py
+++ b/solution.py
@@ -12,7 +12,8 @@
 FINE_STEPS = 32
 LANES = 128
 ROWS = 8
-TABLE_BUDGET = 16 << 20
+TABLE_BUDGET = 4 << 20
+KERNEL_BYTES = 8 << 20
 
 COS_TURN = (
     0.9999999998781397, -19.739208740145937, 64.9393888386778, -85.45665201444898,
@@ -50,15 +51,38 @@
     return column, filled
 
 
-def analysis_kernel(held, counts, weights, waves_ref, grid_hbm, coef_ref, table_ref, values, arrived):
+def analysis_kernel(
+    held, fields,
+    counts_hbm, weights_hbm, waves_hbm, stiffness_hbm, basis_hbm, grid_hbm,
+    coef_ref, table_ref, basis_ref, wave_ref, stiffness_ref, limit_ref,
+    counts, weights, waves, levels, values, arrived,
+):
     owners, pairs, _, _ = coef_ref.shape
     slots = owners * ROWS
     points = grid_hbm.shape[1]
     rows = grid_hbm.shape[0] // pairs
-    fetch = pltpu.make_async_copy(grid_hbm, values, arrived)
-    fetch.start()
-    wave, filled = wave_column(waves_ref, held, slots)
+    needed = [
+        pltpu.make_async_copy(source, target, arrived.at[k])
+        for k, (source, target) in enumerate(
+            [(counts_hbm, counts), (waves_hbm, waves), (weights_hbm, weights),
+             (stiffness_hbm, levels), (grid_hbm, values), (basis_hbm, basis_ref)]
+        )
+    ]
+    for copy in needed:
+        copy.start()
+    for copy in needed[:5]:
+        copy.wait()
+    wave, filled = wave_column(waves, held, slots)
+    wave_ref[...] = jnp.broadcast_to(wave, (slots, LANES))
     lane = lax.broadcasted_iota(jnp.int32, (1, LANES), 1)
+    all_levels = levels.shape[1]
+    own = jnp.concatenate([levels[...], jnp.zeros((1, LANES - all_levels), jnp.float32)], axis=1)
+    own = pltpu.roll(own, (LANES - lax.axis_index("lev") * fields) % LANES, 1)
+    own = jnp.where(lane < fields, own, 0.0)
+    stiffness = own
+    for copy in range(1, 4):
+        stiffness = stiffness + pltpu.roll(own, copy * fields, 1)
+    stiffness_ref[...] = stiffness
     lane_count = jnp.ones((1, LANES), jnp.float32)
     for j in range(pairs):
         lane_count = jnp.where(lane == j, counts[j].astype(jnp.float32), lane_count)
@@ -68,8 +92,10 @@
     )
     steps = wave * lane.astype(jnp.float32)
     blocks = table_ref.shape[2] // LANES
+    position = lax.broadcasted_iota(jnp.int32, (1, points), 1)
     for j in range(pairs):
         count = jnp.full((1, LANES), counts[j].astype(jnp.float32))
+        limit_ref[j : j + 1, :] = count
         inverse = 1.0 / count
         cosine, sine = cos_minus_sin(steps, count, inverse)
         kept = filled & (2.0 * wave < count[:, :1])
@@ -86,9 +112,6 @@
             at = pl.ds(block * LANES, LANES)
             table_ref[j, :slots, at] = cosine.astype(jnp.bfloat16)
             table_ref[j, slots:, at] = sine.astype(jnp.bfloat16)
-    fetch.wait()
-    position = lax.broadcasted_iota(jnp.int32, (1, points), 1)
-    for j in range(pairs):
         inside = jnp.where(position < counts[j], 1.0, 0.0).astype(jnp.bfloat16)
         latitude = values[j * rows : (j + 1) * rows, :] * inside
         product = lax.dot_general(
@@ -97,8 +120,7 @@
             (((1,), (1,)), ((), ())),
             preferred_element_type=jnp.float32,
         )
-        scale = jnp.full((1, 1), weights[j]) / jnp.full((1, 1), counts[j].astype(jnp.float32))
-        product = product * scale
+        product = product * (jnp.full((1, 1), weights[j]) * inverse[:, :1])
         packed = jnp.concatenate(
             [
                 product[:slots],
@@ -108,28 +130,26 @@
             axis=1,
         )
         coef_ref[:, j] = packed.reshape(owners, ROWS, LANES).astype(jnp.bfloat16)
-
-
-def legendre_kernel(held, fields, waves, stiffness_ref, basis_ref, recv_ref, send_ref, fan_in, fan_out):
+    needed[5].wait()
+
+
+def legendre_kernel(held, fields, wave_ref, stiffness_ref, basis_ref, recv_ref, send_ref, fan_in, fan_out):
     owners, pairs, _, _ = recv_ref.shape
     latitudes = owners * pairs
     width = basis_ref.shape[2]
-    first = lax.axis_index("lat") * held
+    first = lax.axis_index("lat") * ROWS
     fan_in[...] = recv_ref[...].astype(jnp.float32).reshape(latitudes * ROWS, LANES)
+    stiffness = stiffness_ref[...]
     lane = lax.broadcasted_iota(jnp.int32, (1, LANES), 1)
-    own = pltpu.roll(stiffness_ref[...], (LANES - lax.axis_index("lev") * fields) % LANES, 1)
-    own = jnp.where(lane < fields, own, 0.0)
-    stiffness = own
-    for copy in range(1, 4):
-        stiffness = stiffness + pltpu.roll(own, copy * fields, 1)
     south = ((lane >= fields) & (lane < 2 * fields)) | (lane >= 3 * fields)
     offset = lax.broadcasted_iota(jnp.int32, (width, 1), 0)
     parity = jnp.where((offset & 1) == 0, 1.0, -1.0)
+    offset = offset.astype(jnp.float32)
     for c in range(held):
-        wave = waves[first + c]
-        degree = (offset + wave).astype(jnp.float32)
+        wave = wave_ref[pl.ds(first + c, 1), :]
+        degree = offset + wave
         factor = 1.0 / (1.0 + stiffness * degree * (degree + 1.0))
-        damping = jnp.where(offset < width - wave, factor, 0.0)
+        damping = jnp.where(degree < float(width), factor, 0.0)
         block = fan_in[pl.ds(c, latitudes, stride=ROWS), :].astype(jnp.bfloat16)
         basis = basis_ref[c]
         spectra = lax.dot_general(
@@ -140,19 +160,19 @@
         )
         scaled = ((spectra + parity * other) * damping).astype(jnp.bfloat16)
         returned = jnp.dot(basis, scaled, preferred_element_type=jnp.float32)
-        returned = returned * jnp.where(wave == 0, 1.0, 2.0)
+        returned = returned * jnp.where(wave == 0.0, 1.0, 2.0)
         fan_out[pl.ds(c, latitudes, stride=ROWS), :] = returned
     for c in range(held, ROWS):
         fan_out[pl.ds(c, latitudes, stride=ROWS), :] = jnp.zeros((latitudes, LANES), jnp.float32)
     send_ref[...] = fan_out[...].reshape(owners, pairs, ROWS, LANES).astype(jnp.bfloat16)
 
 
-def synthesis_kernel(counts, recv_ref, table_ref, grid_hbm, values, left):
+def synthesis_kernel(limit_ref, recv_ref, table_ref, grid_hbm, values, left):
     owners, pairs, _, _ = recv_ref.shape
     slots = owners * ROWS
     points = grid_hbm.shape[1]
     rows = grid_hbm.shape[0] // pairs
-    position = lax.broadcasted_iota(jnp.int32, (1, points), 1)
+    position = lax.broadcasted_iota(jnp.int32, (1, points), 1).astype(jnp.float32)
     copies = []
     for j in range(pairs):
         block = recv_ref[:, j].astype(jnp.float32).reshape(slots, LANES)
@@ -163,7 +183,7 @@
             (((0,), (0,)), ((), ())),
             preferred_element_type=jnp.float32,
         )
-        kept = jnp.where(position < counts[j], product[:, :points], 0.0)
+        kept = jnp.where(position < limit_ref[j : j + 1, :1], product[:, :points], 0.0)
         at = pl.ds(j * rows, rows)
         values[at, :] = kept.astype(jnp.bfloat16)
         copies.append(pltpu.make_async_copy(values.at[at, :], grid_hbm.at[at, :], left.at[j]))
@@ -180,46 +200,67 @@
     slots = owners * ROWS
     rows = 2 * fields
     padded = -(-points // LANES) * LANES
-    smem = pl.BlockSpec(memory_space=pltpu.SMEM)
     vmem = pl.BlockSpec(memory_space=pltpu.VMEM)
-    anywhere = pl.BlockSpec(memory_space=pl.ANY)
+    hbm = pl.BlockSpec(memory_space=pltpu.HBM)
+    limits = pltpu.CompilerParams(vmem_limit_bytes=KERNEL_BYTES)
     exchanged = jax.ShapeDtypeStruct((owners, pairs, ROWS, LANES), jnp.bfloat16)
-    coefficients, tables = pl.pallas_call(
-        functools.partial(analysis_kernel, held),
-        out_shape=(exchanged, jax.ShapeDtypeStruct((pairs, 2 * slots, padded), jnp.bfloat16)),
-        in_specs=[smem, smem, vmem, anywhere],
-        out_specs=(vmem, vmem),
+    coefficients, tables, basis, wave_rows, levels, ends = pl.pallas_call(
+        functools.partial(analysis_kernel, held, fields),
+        out_shape=(
+            exchanged,
+            jax.ShapeDtypeStruct((pairs, 2 * slots, padded), jnp.bfloat16),
+            jax.ShapeDtypeStruct(legendre.shape, legendre.dtype),
+            jax.ShapeDtypeStruct((slots, LANES), jnp.float32),
+            jax.ShapeDtypeStruct((1, LANES), jnp.float32),
+            jax.ShapeDtypeStruct((pairs, LANES), jnp.float32),
+        ),
+        in_specs=[hbm] * 6,
+        out_specs=(vmem,) * 6,
         scratch_shapes=[
+            pltpu.SMEM((pairs,), jnp.int32),
+            pltpu.SMEM((pairs,), jnp.float32),
+            pltpu.VMEM((1, width), jnp.int32),
+            pltpu.VMEM((1, stiffness.shape[0]), jnp.float32),
             pltpu.VMEM((pairs * rows, points), jnp.bfloat16),
-            pltpu.SemaphoreType.DMA,
+            pltpu.SemaphoreType.DMA((6,)),
         ],
+        compiler_params=limits,
         name="analysis",
-    )(point_counts, weights, waves.reshape(1, width), grid.reshape(pairs * rows, points))
+    )(
+        *(
+            pltpu.with_memory_space_constraint(array, pltpu.HBM)
+            for array in (
+                point_counts, weights, waves.reshape(1, width), stiffness.reshape(1, -1), legendre,
+                grid.reshape(pairs * rows, points),
+            )
+        )
+    )
     received = lax.all_to_all(coefficients, "lat", split_axis=0, concat_axis=0, tiled=True)
-    lane_stiffness = jnp.pad(stiffness, (0, LANES - stiffness.shape[0])).reshape(1, LANES)
     synthesised = pl.pallas_call(
         functools.partial(legendre_kernel, held, fields),
         out_shape=exchanged,
-        in_specs=[smem, vmem, vmem, vmem],
+        in_specs=[vmem] * 4,
         out_specs=vmem,
         scratch_shapes=[
             pltpu.VMEM((owners * pairs * ROWS, LANES), jnp.float32),
             pltpu.VMEM((owners * pairs * ROWS, LANES), jnp.float32),
         ],
+        compiler_params=limits,
         name="legendre",
-    )(waves, lane_stiffness, legendre, received)
+    )(wave_rows, levels, basis, received)
     returned = lax.all_to_all(synthesised, "lat", split_axis=0, concat_axis=0, tiled=True)
     result = pl.pallas_call(
         synthesis_kernel,
         out_shape=jax.ShapeDtypeStruct((pairs * rows, points), jnp.bfloat16),
-        in_specs=[smem, vmem, vmem],
-        out_specs=anywhere,
+        in_specs=[vmem] * 3,
+        out_specs=hbm,
         scratch_shapes=[
             pltpu.VMEM((pairs * rows, points), jnp.bfloat16),
             pltpu.SemaphoreType.DMA((pairs,)),
         ],
+        compiler_params=limits,
         name="synthesis",
-    )(point_counts, returned, tables)
+    )(ends, returned, tables)
     return result.reshape(grid.shape)
 
 

time: 38.4 us -> 32.7 us (0.85)
  blocking collectives: 12.3 us -> 28.1 us
  starting transfers between devices: 8.35 us -> 0 us
  waiting for transfers between devices: 7.46 us -> 0 us
  Pallas kernels: 8.1 us -> 4.37 us
  local copies, waits for them, and re-layouts: 1.85 us -> 0 us
    all_to_all x0 -> x1, blocking collectives: none -> 16.8 us  [on_device(): lax.all_to_all(coefficients, 'lat', split_axis=0, concat_axis=0, tiled=True)]
    all_to_all x1 -> x0, starting transfers between devices: 8.35 us -> none  [on_device(): lax.all_to_all(coefficients, 'lat', split_axis=0, concat_axis=0, tiled=True)]
    all_to_all x1 -> x0, waiting for transfers between devices: 7.46 us -> none  [on_device(): lax.all_to_all(coefficients, 'lat', split_axis=0, concat_axis=0, tiled=True)]
    pallas_call x1, Pallas kernels: 2.24 us -> 0.55 us  [on_device(): pl.pallas_call(functools.partial(legendre_kernel, held, fields), out_shap...]
    pallas_call x1, Pallas kernels: 2.77 us -> 1.23 us  [on_device(): pl.pallas_call(synthesis_kernel, out_shape=jax.ShapeDtypeStruct((pairs *...]
    reshape x1 -> x0, local copies, waits for them, and re-layouts: 1.18 us -> none  [on_device(): jnp.pad(stiffness, (0, LANES - stiffness.shape[0])).reshape(1, LANES)]
    all_to_all x1, blocking collectives: 12.3 us -> 11.3 us  [on_device(): lax.all_to_all(synthesised, 'lat', split_axis=0, concat_axis=0, tiled=True)]
    unnamed x2 -> x0, local copies, waits for them, and re-layouts: 0.68 us -> none
  transfers between devices with their start and end apart: 1 -> 0, of which waited for: 1 -> 0; matrix products, arithmetic and copies ran while one was open for 3% -> 0% of each run, Pallas kernels for 0% -> 0%
where the time goes in v2:
time: 32.7 us; the launch traced here: 32.5 us
  blocking collectives  28.1 us (86%)
  Pallas kernels  4.37 us (13%)
    all_to_all x1, blocking collectives, on_device(): lax.all_to_all(coefficients, 'lat', split_axis=0, concat_axis=0, tiled=True)  16.8 us
    all_to_all x1, blocking collectives, on_device(): lax.all_to_all(synthesised, 'lat', split_axis=0, concat_axis=0, tiled=True)  11.3 us
    pallas_call x1, Pallas kernels, on_device(): pl.pallas_call(functools.partial(analysis_kernel, held, fields), out_shap...  2.59 us
    pallas_call x1, Pallas kernels, on_device(): pl.pallas_call(synthesis_kernel, out_shape=jax.ShapeDtypeStruct((pairs *...  1.23 us

profile of v2, /device:TPU:0, one launch (start us, length us, event | category | flops | bytes accessed | tf_op | source)
XLA Modules:
  0.0 32.5 jit_solution(956999697001372095)
XLA Ops:
  0.0 2.6 %analysis.1 = (bf16[16,6,8,128]{3,2,1,0:T(8,128)(2,1)S(1)}, bf16[6,256,512]{2,1,0:T(8,128)(2,1)S(1)}, bf16[6,96,96]{2,1,0:T(8,128)(2,1)S(1)}, f32[128,128]{1,0:T...) custom-call(s32[6]{0:T(128)} %counts_hbm.1, f32[6]{0:T(128)} %weights_hbm.1, s32[1,96]{1,0:T(1,128)} %bitcast.5, ...), custom_call_target="tpu_custom_call" | custom-call | tf_op jit(solution)/shard_map/analysis/pallas_call | solution.py:207
  2.6 16.8 %all_to_all.10.recv_ref = bf16[16,6,8,128]{3,2,1,0:T(8,128)(2,1)S(1)} all-to-all(bf16[16,6,8,128]{3,2,1,0:T(8,128)(2,1)S(1)} %get-tuple-element.15), channel_id=1, replica_groups=mesh['lat'=16,'lev'=2] {'lat'}, dimensions={0} | all-to-all | bytes 393216 | tf_op jit(solution)/shard_map/all_to_all | solution.py:238
  19.4 0.6 %legendre.1 = bf16[16,6,8,128]{3,2,1,0:T(8,128)(2,1)S(1)} custom-call(f32[128,128]{1,0:T(8,128)S(1)} %get-tuple-element.12.wave_ref, f32[1,128]{1,0:T(1,128)S(1)} %get-tuple-element.13.stiffness_ref, bf16[6,96,96]{2,1,0:T(8,128)(2,1)S(1)} %get-tuple-element.14.basis_ref, bf16[16,6,8,128]{3,2,1,0:T(8,128)(2,1)S(1)} %all_to_all.10.recv_ref), custom_call_target="tpu_custom_call" | custom-call | tf_op jit(solution)/shard_map/legendre/pallas_call | solution.py:239
  19.9 11.3 %all_to_all.11.recv_ref = bf16[16,6,8,128]{3,2,1,0:T(8,128)(2,1)S(1)} all-to-all(bf16[16,6,8,128]{3,2,1,0:T(8,128)(2,1)S(1)} %legendre.1), channel_id=1, replica_groups=mesh['lat'=16,'lev'=2] {'lat'}, dimensions={0} | all-to-all | bytes 393216 | tf_op jit(solution)/shard_map/all_to_all | solution.py:251
  31.2 1.2 %synthesis.1 = bf16[288,400]{1,0:T(8,128)(2,1)} custom-call(f32[6,128]{1,0:T(8,128)S(1)} %get-tuple-element.11.limit_ref, bf16[16,6,8,128]{3,2,1,0:T(8,128)(2,1)S(1)} %all_to_all.11.recv_ref, bf16[6,256,512]{2,1,0:T(8,128)(2,1)S(1)} %get-tuple-element.16.table_ref), custom_call_target="tpu_custom_call" | custom-call | tf_op jit(solution)/shard_map/synthesis/pallas_call | solution.py:252

commit v3 on v2

--- a/solution.py
+++ b/solution.py
@@ -12,6 +12,7 @@
 FINE_STEPS = 32
 LANES = 128
 ROWS = 8
+HALF = 4
 TABLE_BUDGET = 4 << 20
 KERNEL_BYTES = 8 << 20
 
@@ -43,46 +44,90 @@
     width = waves_ref.shape[1]
     row = lax.broadcasted_iota(jnp.int32, (slots, width), 0)
     lane = lax.broadcasted_iota(jnp.int32, (slots, width), 1)
-    place = row & (ROWS - 1)
-    chosen = ((row >> 3) * held + place == lane) & (place < held)
+    place = row & (HALF - 1)
+    chosen = ((row >> 2) * held + place == lane) & (place < held)
     waves = jnp.broadcast_to(waves_ref[...].astype(jnp.float32), (slots, width))
     column = jnp.sum(jnp.where(chosen, waves, 0.0), axis=1, keepdims=True)
-    filled = (lax.broadcasted_iota(jnp.int32, (slots, 1), 0) & (ROWS - 1)) < held
+    filled = (lax.broadcasted_iota(jnp.int32, (slots, 1), 0) & (HALF - 1)) < held
     return column, filled
+
+
+def segments(start, length):
+    done = 0
+    while done < length:
+        block, lane = divmod(start + done, LANES)
+        size = min(length - done, LANES - lane)
+        yield block, lane, done, size
+        done += size
+
+
+def turn(x, shift, axis):
+    shift %= x.shape[axis]
+    return pltpu.roll(x, shift, axis) if shift else x
+
+
+def fold_rest(whole, part, held, rest):
+    sublane = lax.broadcasted_iota(jnp.int32, (1, ROWS, LANES), 1) & (HALF - 1)
+    lane = lax.broadcasted_iota(jnp.int32, (1, ROWS, LANES), 2)
+    for c in range(held):
+        moved = turn(turn(part, HALF - 1 - c, 1), c * rest, 2)
+        here = (sublane == HALF - 1) & (lane >= c * rest) & (lane < (c + 1) * rest)
+        whole = jnp.where(here, moved, whole)
+    return whole
+
+
+def unfold_rest(whole, held, rest):
+    sublane = lax.broadcasted_iota(jnp.int32, (1, ROWS, LANES), 1) & (HALF - 1)
+    part = whole
+    for c in range(held):
+        part = jnp.where(sublane == c, turn(turn(whole, c + 1 - HALF, 1), -c * rest, 2), part)
+    return part
 
 
 def analysis_kernel(
     held, fields,
     counts_hbm, weights_hbm, waves_hbm, stiffness_hbm, basis_hbm, grid_hbm,
     coef_ref, table_ref, basis_ref, wave_ref, stiffness_ref, limit_ref,
-    counts, weights, waves, levels, values, arrived,
+    counts, weights, waves, levels, values, given, widened, arrived,
 ):
-    owners, pairs, _, _ = coef_ref.shape
-    slots = owners * ROWS
+    owners, blocks, _, _ = coef_ref.shape
+    pairs = table_ref.shape[0]
+    slots = owners * HALF
     points = grid_hbm.shape[1]
     rows = grid_hbm.shape[0] // pairs
+    rest = pairs * rows - blocks * LANES
+    groups = slots // ROWS
+    own_basis = basis_hbm.at[pl.ds(lax.axis_index("lev") * held, held)]
     needed = [
         pltpu.make_async_copy(source, target, arrived.at[k])
         for k, (source, target) in enumerate(
             [(counts_hbm, counts), (waves_hbm, waves), (weights_hbm, weights),
-             (stiffness_hbm, levels), (grid_hbm, values), (basis_hbm, basis_ref)]
+             (stiffness_hbm, levels), (grid_hbm, values), (own_basis, given)]
         )
     ]
     for copy in needed:
         copy.start()
-    for copy in needed[:5]:
+    for copy in needed:
         copy.wait()
     wave, filled = wave_column(waves, held, slots)
     wave_ref[...] = jnp.broadcast_to(wave, (slots, LANES))
+    latitudes = basis_ref.shape[1]
+    shards = latitudes // pairs
+    widened[...] = given[...].astype(jnp.float32)
+    for c in range(held):
+        for j in range(pairs):
+            basis_ref[c, j * shards : (j + 1) * shards, :] = widened[
+                c, pl.ds(j, shards, stride=pairs), :
+            ].astype(jnp.bfloat16)
     lane = lax.broadcasted_iota(jnp.int32, (1, LANES), 1)
     all_levels = levels.shape[1]
-    own = jnp.concatenate([levels[...], jnp.zeros((1, LANES - all_levels), jnp.float32)], axis=1)
-    own = pltpu.roll(own, (LANES - lax.axis_index("lev") * fields) % LANES, 1)
-    own = jnp.where(lane < fields, own, 0.0)
-    stiffness = own
-    for copy in range(1, 4):
-        stiffness = stiffness + pltpu.roll(own, copy * fields, 1)
-    stiffness_ref[...] = stiffness
+    padded = jnp.concatenate([levels[...], jnp.zeros((1, LANES - all_levels), jnp.float32)], axis=1)
+    for shard in range(all_levels // fields):
+        own = jnp.where(lane < fields, turn(padded, -shard * fields, 1), 0.0)
+        stiffness = own
+        for copy in range(1, 4):
+            stiffness = stiffness + turn(own, copy * fields, 1)
+        stiffness_ref[shard : shard + 1, :] = stiffness
     lane_count = jnp.ones((1, LANES), jnp.float32)
     for j in range(pairs):
         lane_count = jnp.where(lane == j, counts[j].astype(jnp.float32), lane_count)
@@ -91,8 +136,8 @@
         jnp.broadcast_to(wave * float(LANES), (slots, LANES)), lane_count, lane_inverse
     )
     steps = wave * lane.astype(jnp.float32)
-    blocks = table_ref.shape[2] // LANES
     position = lax.broadcasted_iota(jnp.int32, (1, points), 1)
+    real, imaginary = [], []
     for j in range(pairs):
         count = jnp.full((1, LANES), counts[j].astype(jnp.float32))
         limit_ref[j : j + 1, :] = count
@@ -103,7 +148,7 @@
         sine = jnp.where(kept, sine, 0.0)
         block_cos = turn_cos[:, j : j + 1]
         block_sin = turn_sin[:, j : j + 1]
-        for block in range(blocks):
+        for block in range(table_ref.shape[2] // LANES):
             if block > 0:
                 cosine, sine = (
                     cosine * block_cos - sine * block_sin,
@@ -121,67 +166,146 @@
             preferred_element_type=jnp.float32,
         )
         product = product * (jnp.full((1, 1), weights[j]) * inverse[:, :1])
-        packed = jnp.concatenate(
-            [
-                product[:slots],
-                product[slots:],
-                jnp.zeros((slots, LANES - 2 * rows), jnp.float32),
-            ],
-            axis=1,
-        )
-        coef_ref[:, j] = packed.reshape(owners, ROWS, LANES).astype(jnp.bfloat16)
-    needed[5].wait()
-
-
-def legendre_kernel(held, fields, wave_ref, stiffness_ref, basis_ref, recv_ref, send_ref, fan_in, fan_out):
-    owners, pairs, _, _ = recv_ref.shape
-    latitudes = owners * pairs
-    width = basis_ref.shape[2]
-    first = lax.axis_index("lat") * ROWS
-    fan_in[...] = recv_ref[...].astype(jnp.float32).reshape(latitudes * ROWS, LANES)
-    stiffness = stiffness_ref[...]
-    lane = lax.broadcasted_iota(jnp.int32, (1, LANES), 1)
-    south = ((lane >= fields) & (lane < 2 * fields)) | (lane >= 3 * fields)
+        real.append(product[:slots])
+        imaginary.append(product[slots:])
+    tail = [jnp.zeros((slots, LANES - rest), jnp.float32)] if rest else []
+    parts = []
+    for pieces in (real, imaginary):
+        whole = jnp.concatenate(pieces + tail, axis=1)
+        cut = [
+            whole[:, block * LANES : (block + 1) * LANES].reshape(groups, ROWS, LANES)
+            for block in range(whole.shape[1] // LANES)
+        ]
+        if rest:
+            cut[-2] = fold_rest(cut[-2], cut[-1], held, rest)
+        parts.append(cut)
+    low = lax.broadcasted_iota(jnp.int32, (1, ROWS, LANES), 1) < HALF
+    for block in range(blocks):
+        first, second = parts[0][block], parts[1][block]
+        even = jnp.where(low, first, turn(second, HALF, 1))
+        odd = jnp.where(low, turn(first, HALF, 1), second)
+        both = jnp.stack([even, odd], axis=1).reshape(owners, ROWS, LANES)
+        coef_ref[:, block] = both.astype(jnp.bfloat16)
+
+
+def legendre_kernel(
+    held, fields, wave_ref, stiffness_ref, basis_ref, recv_ref, send_ref, fan_in, fan_out
+):
+    owners, blocks, _, _ = recv_ref.shape
+    latitudes, width = basis_ref.shape[1:]
+    shards = stiffness_ref.shape[0]
+    senders = owners // shards
+    pairs = latitudes // senders
+    rows = 2 * fields
+    rest = pairs * rows - blocks * LANES
+    first = (lax.axis_index("lat") * shards + lax.axis_index("lev")) * HALF
+    fan_in[...] = recv_ref[...].astype(jnp.float32).reshape(owners * blocks * ROWS, LANES)
+
+    def chunk_rows(shard, block, row):
+        return pl.ds((shard * blocks + block) * ROWS + row, senders, stride=shards * blocks * ROWS)
+
+    def home(part, c, block, lane):
+        if block == blocks:
+            return part * HALF + HALF - 1, block - 1, c * rest + lane
+        return part * HALF + c, block, lane
+
+    lane_at = lax.broadcasted_iota(jnp.int32, (1, LANES), 1)
+    south = ((lane_at >= fields) & (lane_at < 2 * fields)) | (lane_at >= 3 * fields)
     offset = lax.broadcasted_iota(jnp.int32, (width, 1), 0)
     parity = jnp.where((offset & 1) == 0, 1.0, -1.0)
     offset = offset.astype(jnp.float32)
+    folded = {}
     for c in range(held):
         wave = wave_ref[pl.ds(first + c, 1), :]
         degree = offset + wave
-        factor = 1.0 / (1.0 + stiffness * degree * (degree + 1.0))
-        damping = jnp.where(degree < float(width), factor, 0.0)
-        block = fan_in[pl.ds(c, latitudes, stride=ROWS), :].astype(jnp.bfloat16)
         basis = basis_ref[c]
+        sides = []
+        for shard in range(shards):
+            strips = []
+            for j in range(pairs):
+                strip = jnp.zeros((senders, LANES), jnp.float32)
+                for part in range(2):
+                    for block, lane, place, size in segments(j * rows, rows):
+                        row, block, lane = home(part, c, block, lane)
+                        source = fan_in[chunk_rows(shard, block, row), :]
+                        target = part * rows + place
+                        here = (lane_at >= target) & (lane_at < target + size)
+                        strip = jnp.where(here, turn(source, target - lane, 1), strip)
+                strips.append(strip.astype(jnp.bfloat16))
+            sides.append(jnp.concatenate(strips, axis=0))
         spectra = lax.dot_general(
-            basis, block, (((0,), (0,)), ((), ())), preferred_element_type=jnp.float32
-        )
-        other = jnp.where(
-            south, pltpu.roll(spectra, fields, 1), pltpu.roll(spectra, LANES - fields, 1)
-        )
-        scaled = ((spectra + parity * other) * damping).astype(jnp.bfloat16)
-        returned = jnp.dot(basis, scaled, preferred_element_type=jnp.float32)
-        returned = returned * jnp.where(wave == 0.0, 1.0, 2.0)
-        fan_out[pl.ds(c, latitudes, stride=ROWS), :] = returned
-    for c in range(held, ROWS):
-        fan_out[pl.ds(c, latitudes, stride=ROWS), :] = jnp.zeros((latitudes, LANES), jnp.float32)
-    send_ref[...] = fan_out[...].reshape(owners, pairs, ROWS, LANES).astype(jnp.bfloat16)
-
-
-def synthesis_kernel(limit_ref, recv_ref, table_ref, grid_hbm, values, left):
-    owners, pairs, _, _ = recv_ref.shape
-    slots = owners * ROWS
+            basis,
+            jnp.concatenate(sides, axis=1),
+            (((0,), (0,)), ((), ())),
+            preferred_element_type=jnp.float32,
+        )
+        scaled = []
+        for shard in range(shards):
+            side = spectra[:, shard * LANES : (shard + 1) * LANES]
+            factor = 1.0 / (1.0 + stiffness_ref[shard : shard + 1, :] * degree * (degree + 1.0))
+            damping = jnp.where(degree < float(width), factor, 0.0)
+            other = jnp.where(south, turn(side, fields, 1), turn(side, -fields, 1))
+            scaled.append(((side + parity * other) * damping).astype(jnp.bfloat16))
+        returned = jnp.dot(
+            basis, jnp.concatenate(scaled, axis=1), preferred_element_type=jnp.float32
+        )
+        weight = jnp.where(wave == 0.0, 1.0, 2.0)
+        for shard in range(shards):
+            side = returned[:, shard * LANES : (shard + 1) * LANES] * weight
+            for part in range(2):
+                built = {}
+                for j in range(pairs):
+                    strip = side[j * senders : (j + 1) * senders]
+                    for block, lane, place, size in segments(j * rows, rows):
+                        row, block, lane = home(part, c, block, lane)
+                        key = (shard, block, row)
+                        here = (lane_at >= lane) & (lane_at < lane + size)
+                        moved = turn(strip, lane - part * rows - place, 1)
+                        held_in = folded if row % HALF == HALF - 1 else built
+                        before = held_in.get(key, jnp.zeros((senders, LANES), jnp.float32))
+                        held_in[key] = jnp.where(here, moved, before)
+                for key, value in built.items():
+                    fan_out[chunk_rows(*key), :] = value
+    empty = jnp.zeros((senders, LANES), jnp.float32)
+    for shard in range(shards):
+        for block in range(blocks):
+            for part in range(2):
+                for place in range(held, HALF):
+                    key = (shard, block, part * HALF + place)
+                    fan_out[chunk_rows(*key), :] = folded.get(key, empty)
+    send_ref[...] = fan_out[...].reshape(owners, blocks, ROWS, LANES).astype(jnp.bfloat16)
+
+
+def synthesis_kernel(held, limit_ref, recv_ref, table_ref, grid_hbm, values, left):
+    owners, blocks, _, _ = recv_ref.shape
+    pairs = table_ref.shape[0]
+    slots = owners * HALF
     points = grid_hbm.shape[1]
     rows = grid_hbm.shape[0] // pairs
+    rest = pairs * rows - blocks * LANES
+    groups = slots // ROWS
+    low = lax.broadcasted_iota(jnp.int32, (1, ROWS, LANES), 1) < HALF
+    parts = ([], [])
+    for block in range(blocks):
+        both = recv_ref[:, block].astype(jnp.float32).reshape(groups, 2, ROWS, LANES)
+        even, odd = both[:, 0], both[:, 1]
+        parts[0].append(jnp.where(low, even, turn(odd, HALF, 1)))
+        parts[1].append(jnp.where(low, turn(even, HALF, 1), odd))
+    if rest:
+        for part in parts:
+            part.append(unfold_rest(part[-1], held, rest))
+    operand = jnp.concatenate(
+        [
+            jnp.concatenate([part[block].reshape(slots, LANES) for part in parts], axis=0).T
+            for block in range(len(parts[0]))
+        ],
+        axis=0,
+    ).astype(jnp.bfloat16)
     position = lax.broadcasted_iota(jnp.int32, (1, points), 1).astype(jnp.float32)
     copies = []
     for j in range(pairs):
-        block = recv_ref[:, j].astype(jnp.float32).reshape(slots, LANES)
-        operand = jnp.concatenate([block[:, :rows], block[:, rows : 2 * rows]], axis=0)
-        product = lax.dot_general(
-            operand.astype(jnp.bfloat16),
-            table_ref[j],
-            (((0,), (0,)), ((), ())),
-            preferred_element_type=jnp.float32,
+        product = jnp.dot(
+            operand[j * rows : (j + 1) * rows], table_ref[j], preferred_element_type=jnp.float32
         )
         kept = jnp.where(position < limit_ref[j : j + 1, :1], product[:, :points], 0.0)
         at = pl.ds(j * rows, rows)
@@ -192,26 +316,29 @@
         copy.wait()
 
 
-def on_device(grid, point_counts, waves, legendre, weights, stiffness):
+def on_device(mesh, grid, point_counts, waves, legendre, weights, stiffness):
     pairs, _, fields, points = grid.shape
-    held = legendre.shape[0]
     width = waves.shape[0]
-    owners = width // held
-    slots = owners * ROWS
+    shards = mesh.shape["lev"]
+    owners = mesh.shape["lat"] * shards
+    held = width // owners
+    slots = owners * HALF
     rows = 2 * fields
     padded = -(-points // LANES) * LANES
+    blocks = pairs * rows // LANES
+    own_basis = (held,) + legendre.shape[1:]
     vmem = pl.BlockSpec(memory_space=pltpu.VMEM)
     hbm = pl.BlockSpec(memory_space=pltpu.HBM)
     limits = pltpu.CompilerParams(vmem_limit_bytes=KERNEL_BYTES)
-    exchanged = jax.ShapeDtypeStruct((owners, pairs, ROWS, LANES), jnp.bfloat16)
+    exchanged = jax.ShapeDtypeStruct((owners, blocks, ROWS, LANES), jnp.bfloat16)
     coefficients, tables, basis, wave_rows, levels, ends = pl.pallas_call(
         functools.partial(analysis_kernel, held, fields),
         out_shape=(
             exchanged,
             jax.ShapeDtypeStruct((pairs, 2 * slots, padded), jnp.bfloat16),
-            jax.ShapeDtypeStruct(legendre.shape, legendre.dtype),
+            jax.ShapeDtypeStruct(own_basis, jnp.bfloat16),
             jax.ShapeDtypeStruct((slots, LANES), jnp.float32),
-            jax.ShapeDtypeStruct((1, LANES), jnp.float32),
+            jax.ShapeDtypeStruct((shards, LANES), jnp.float32),
             jax.ShapeDtypeStruct((pairs, LANES), jnp.float32),
         ),
         in_specs=[hbm] * 6,
@@ -222,6 +349,8 @@
             pltpu.VMEM((1, width), jnp.int32),
             pltpu.VMEM((1, stiffness.shape[0]), jnp.float32),
             pltpu.VMEM((pairs * rows, points), jnp.bfloat16),
+            pltpu.VMEM(own_basis, jnp.bfloat16),
+            pltpu.VMEM(own_basis, jnp.float32),
             pltpu.SemaphoreType.DMA((6,)),
         ],
         compiler_params=limits,
@@ -235,22 +364,23 @@
             )
         )
     )
-    received = lax.all_to_all(coefficients, "lat", split_axis=0, concat_axis=0, tiled=True)
+    everyone = ("lat", "lev")
+    received = lax.all_to_all(coefficients, everyone, split_axis=0, concat_axis=0, tiled=True)
     synthesised = pl.pallas_call(
         functools.partial(legendre_kernel, held, fields),
         out_shape=exchanged,
         in_specs=[vmem] * 4,
         out_specs=vmem,
         scratch_shapes=[
-            pltpu.VMEM((owners * pairs * ROWS, LANES), jnp.float32),
-            pltpu.VMEM((owners * pairs * ROWS, LANES), jnp.float32),
+            pltpu.VMEM((owners * blocks * ROWS, LANES), jnp.float32),
+            pltpu.VMEM((owners * blocks * ROWS, LANES), jnp.float32),
         ],
         compiler_params=limits,
         name="legendre",
     )(wave_rows, levels, basis, received)
-    returned = lax.all_to_all(synthesised, "lat", split_axis=0, concat_axis=0, tiled=True)
+    returned = lax.all_to_all(synthesised, everyone, split_axis=0, concat_axis=0, tiled=True)
     result = pl.pallas_call(
-        synthesis_kernel,
+        functools.partial(synthesis_kernel, held),
         out_shape=jax.ShapeDtypeStruct((pairs * rows, points), jnp.bfloat16),
         in_specs=[vmem] * 3,
         out_specs=hbm,
@@ -375,16 +505,22 @@
     return lax.map(synthesise, (returned, matrices, twist_cos, twist_sin, point_counts))
 
 
-def fits_on_chip(mesh, grid, legendre, stiffness):
-    owners, levels = mesh.shape["lat"], mesh.shape["lev"]
-    pairs, fields = grid.shape[0] // owners, grid.shape[2] // levels
-    held = legendre.shape[0] // owners
-    table_bytes = 4 * pairs * owners * ROWS * grid.shape[3]
+def fits_on_chip(mesh, grid, waves, stiffness):
+    shards = mesh.shape["lev"]
+    owners = mesh.shape["lat"] * shards
+    pairs, fields = grid.shape[0] // mesh.shape["lat"], grid.shape[2] // shards
+    held = waves.shape[0] // owners
+    lanes = 2 * pairs * fields
     return (
-        table_bytes <= TABLE_BUDGET
-        and held <= ROWS
+        waves.shape[0] % owners == 0
+        and 4 * pairs * owners * HALF * grid.shape[3] <= TABLE_BUDGET
+        and held < HALF
+        and lanes >= LANES
+        and held * (lanes % LANES) <= LANES
         and 4 * fields <= LANES
         and fields % ROWS == 0
+        and owners * HALF % (2 * ROWS) == 0
+        and mesh.shape["lat"] % (2 * ROWS) == 0
         and stiffness.shape[0] <= LANES
     )
 
@@ -394,7 +530,8 @@
     out_specs = P("lat", None, "lev", None)
 
     def program(grid, point_counts, waves, legendre, weights, stiffness):
-        body = on_device if fits_on_chip(mesh, grid, legendre, stiffness) else on_device_blocked
+        fits = fits_on_chip(mesh, grid, waves, stiffness)
+        body = functools.partial(on_device, mesh) if fits else on_device_blocked
         return jax.shard_map(
             body, mesh=mesh, in_specs=in_specs, out_specs=out_specs, check_vma=False
         )(grid, point_counts, waves, legendre, weights, stiffness)

time: 32.7 us -> 30.2 us (0.924)
  blocking collectives: 28.1 us -> 25.3 us
    all_to_all x2, blocking collectives: 28.1 us -> 25.3 us  [the longest x1 15.3 us: on_device(): lax.all_to_all(coefficients, everyone, split_axis=0, concat_axis=0, tiled...]
where the time goes in v3:
time: 30.2 us; the launch traced here: 30 us
  blocking collectives  25.3 us (84%)
  Pallas kernels  4.65 us (15%)
    all_to_all x1, blocking collectives, on_device(): lax.all_to_all(coefficients, everyone, split_axis=0, concat_axis=0, tiled...  15.3 us
    all_to_all x1, blocking collectives, on_device(): lax.all_to_all(synthesised, everyone, split_axis=0, concat_axis=0, tiled=...  9.97 us
    pallas_call x1, Pallas kernels, on_device(): pl.pallas_call(functools.partial(analysis_kernel, held, fields), out_shap...  2.7 us
    pallas_call x1, Pallas kernels, on_device(): pl.pallas_call(functools.partial(synthesis_kernel, held), out_shape=jax.S...  1.1 us
    pallas_call x1, Pallas kernels, on_device(): pl.pallas_call(functools.partial(legendre_kernel, held, fields), out_shap...  0.85 us

profile of v3, /device:TPU:0, one launch (start us, length us, event | category | flops | bytes accessed | tf_op | source)
XLA Modules:
  0.0 30.0 jit_solution(5722836719353879351)
XLA Ops:
  0.0 2.7 %analysis.1 = (bf16[32,2,8,128]{3,2,1,0:T(8,128)(2,1)S(1)}, bf16[6,256,512]{2,1,0:T(8,128)(2,1)S(1)}, bf16[3,96,96]{2,1,0:T(8,128)(2,1)S(1)}, f32[128,128]{1,0:T...) custom-call(s32[6]{0:T(128)} %counts_hbm.1, f32[6]{0:T(128)} %weights_hbm.1, s32[1,96]{1,0:T(1,128)} %bitcast.5, ...), custom_call_target="tpu_custom_call" | custom-call | tf_op jit(solution)/shard_map/analysis/pallas_call | solution.py:334
  2.7 15.3 %all_to_all.10.recv_ref = bf16[32,2,8,128]{3,2,1,0:T(8,128)(2,1)S(1)} all-to-all(bf16[32,2,8,128]{3,2,1,0:T(8,128)(2,1)S(1)} %get-tuple-element.15), channel_id=1, replica_groups=mesh['lat'=16,'lev'=2] {'lat','lev'}, dimensions={0} | all-to-all | bytes 262144 | tf_op jit(solution)/shard_map/all_to_all | solution.py:368
  18.0 0.8 %legendre.1 = bf16[32,2,8,128]{3,2,1,0:T(8,128)(2,1)S(1)} custom-call(f32[128,128]{1,0:T(8,128)S(1)} %get-tuple-element.12.wave_ref, f32[2,128]{1,0:T(2,128)S(1)} %get-tuple-element.13.stiffness_ref, bf16[3,96,96]{2,1,0:T(8,128)(2,1)S(1)} %get-tuple-element.14.basis_ref, bf16[32,2,8,128]{3,2,1,0:T(8,128)(2,1)S(1)} %all_to_all.10.recv_ref), custom_call_target="tpu_custom_call" | custom-call | tf_op jit(solution)/shard_map/legendre/pallas_call | solution.py:369
  18.9 10.0 %all_to_all.11.recv_ref = bf16[32,2,8,128]{3,2,1,0:T(8,128)(2,1)S(1)} all-to-all(bf16[32,2,8,128]{3,2,1,0:T(8,128)(2,1)S(1)} %legendre.1), channel_id=1, replica_groups=mesh['lat'=16,'lev'=2] {'lat','lev'}, dimensions={0} | all-to-all | bytes 262144 | tf_op jit(solution)/shard_map/all_to_all | solution.py:381
  28.9 1.1 %synthesis.1 = bf16[288,400]{1,0:T(8,128)(2,1)} custom-call(f32[6,128]{1,0:T(8,128)S(1)} %get-tuple-element.11.limit_ref, bf16[32,2,8,128]{3,2,1,0:T(8,128)(2,1)S(1)} %all_to_all.11.recv_ref, bf16[6,256,512]{2,1,0:T(8,128)(2,1)S(1)} %get-tuple-element.16.table_ref), custom_call_target="tpu_custom_call" | custom-call | tf_op jit(solution)/shard_map/synthesis/pallas_call | solution.py:382

commit v4 on v2

--- a/solution.py
+++ b/solution.py
@@ -39,152 +39,312 @@
     return polynomial(COS_TURN, square), -turn * polynomial(SIN_TURN, square)
 
 
-def wave_column(waves_ref, held, slots):
+def slot_choice(waves_ref, held, first, slots):
     width = waves_ref.shape[1]
+    owners = slots // ROWS
     row = lax.broadcasted_iota(jnp.int32, (slots, width), 0)
     lane = lax.broadcasted_iota(jnp.int32, (slots, width), 1)
     place = row & (ROWS - 1)
-    chosen = ((row >> 3) * held + place == lane) & (place < held)
-    waves = jnp.broadcast_to(waves_ref[...].astype(jnp.float32), (slots, width))
+    owner = (row >> 3) + first
+    owner = jnp.where(owner >= owners, owner - owners, owner)
+    chosen = (owner * held + place == lane) & (place < held)
+    waves = jnp.broadcast_to(waves_ref[...].astype(jnp.float32) + 1.0, (slots, width))
     column = jnp.sum(jnp.where(chosen, waves, 0.0), axis=1, keepdims=True)
-    filled = (lax.broadcasted_iota(jnp.int32, (slots, 1), 0) & (ROWS - 1)) < held
-    return column, filled
+    mode = lax.broadcasted_iota(jnp.int32, (slots, LANES), 1).astype(jnp.float32) + 1.0
+    return jnp.where(mode == column, 1.0, 0.0).astype(jnp.bfloat16)
+
+
+def segments(start, length):
+    done = 0
+    while done < length:
+        block, lane = divmod(start + done, LANES)
+        size = min(length - done, LANES - lane)
+        yield block, lane, done, size
+        done += size
+
+
+def turn(x, shift, axis):
+    shift %= x.shape[axis]
+    return pltpu.roll(x, shift, axis) if shift else x
+
+
+def lane_row(lane, pieces, rows):
+    out = []
+    for block in range(-(-len(pieces) * rows // LANES)):
+        total = jnp.zeros((1, LANES), jnp.float32)
+        for j, piece in enumerate(pieces):
+            start, stop = j * rows - block * LANES, (j + 1) * rows - block * LANES
+            if start < LANES and stop > 0:
+                total = jnp.where((lane >= start) & (lane < stop), piece, total)
+        out.append(total)
+    return out
+
+
+def rest_home(c, held, rest):
+    fit = LANES // rest
+    return held + c // fit, (c % fit) * rest
+
+
+def fold_rest(whole, part, held, rest):
+    sublane = lax.broadcasted_iota(jnp.int32, (1, ROWS, LANES), 1)
+    lane = lax.broadcasted_iota(jnp.int32, (1, ROWS, LANES), 2)
+    for c in range(held):
+        row, start = rest_home(c, held, rest)
+        moved = turn(turn(part, row - c, 1), start, 2)
+        here = (sublane == row) & (lane >= start) & (lane < start + rest)
+        whole = jnp.where(here, moved, whole)
+    return whole
+
+
+def unfold_rest(whole, held, rest):
+    sublane = lax.broadcasted_iota(jnp.int32, (1, ROWS, LANES), 1)
+    part = whole
+    for c in range(held):
+        row, start = rest_home(c, held, rest)
+        part = jnp.where(sublane == c, turn(turn(whole, c - row, 1), -start, 2), part)
+    return part
+
+
+def fill_tables(table_ref, width, least):
+    candidates, _, padded = table_ref.shape
+    blocks = padded // LANES
+    sublane = lax.broadcasted_iota(jnp.int32, (ROWS, LANES), 0)
+    lane = lax.broadcasted_iota(jnp.int32, (ROWS, LANES), 1)
+    strides = (ROWS * (sublane * LANES + lane)).astype(jnp.float32)
+    steps = [(sublane * (lane + b * LANES)).astype(jnp.float32) for b in range(blocks)]
+    for i in range(candidates):
+        count = jnp.full((1, LANES), (least + 4 * i).astype(jnp.float32))
+        inverse = 1.0 / count
+        stride_cos, stride_sin = cos_minus_sin(strides, count, inverse)
+        for b in range(blocks):
+            turn_cos, turn_sin = stride_cos[b : b + 1], stride_sin[b : b + 1]
+            twice = turn_cos + turn_cos
+            cosine, sine = cos_minus_sin(steps[b], count, inverse)
+            cosines = [cosine, cosine * turn_cos - sine * turn_sin]
+            sines = [sine, sine * turn_cos + cosine * turn_sin]
+            while len(cosines) * ROWS < width:
+                cosines.append(twice * cosines[-1] - cosines[-2])
+                sines.append(twice * sines[-1] - sines[-2])
+            at = pl.ds(b * LANES, LANES)
+            table_ref[i, :width, at] = jnp.concatenate(cosines, axis=0).astype(jnp.bfloat16)
+            table_ref[i, width:, at] = jnp.concatenate(sines, axis=0).astype(jnp.bfloat16)
+
+
+def least_count(pairs):
+    return 4 * pairs * lax.axis_index("lat") + 16
+
+
+def candidate_of(count, j, least):
+    return j + jnp.clip((count - least - 4 * j) >> 2, 0, 1)
 
 
 def analysis_kernel(
-    held, fields,
+    held, fields, first,
     counts_hbm, weights_hbm, waves_hbm, stiffness_hbm, basis_hbm, grid_hbm,
-    coef_ref, table_ref, basis_ref, wave_ref, stiffness_ref, limit_ref,
-    counts, weights, waves, levels, values, arrived,
+    coef_ref, table_ref, choice_ref, basis_ref, wave_ref, stiffness_ref, limit_ref,
+    counts, weights, waves, levels, values, given, widened, arrived,
 ):
-    owners, pairs, _, _ = coef_ref.shape
+    owners, blocks = coef_ref.shape[:2]
+    pairs = limit_ref.shape[0]
     slots = owners * ROWS
+    width = basis_ref.shape[2]
     points = grid_hbm.shape[1]
     rows = grid_hbm.shape[0] // pairs
+    rest = pairs * rows - blocks * LANES
     needed = [
         pltpu.make_async_copy(source, target, arrived.at[k])
         for k, (source, target) in enumerate(
             [(counts_hbm, counts), (waves_hbm, waves), (weights_hbm, weights),
-             (stiffness_hbm, levels), (grid_hbm, values), (basis_hbm, basis_ref)]
+             (stiffness_hbm, levels), (grid_hbm, values), (basis_hbm, given)]
         )
     ]
     for copy in needed:
         copy.start()
-    for copy in needed[:5]:
+    least = least_count(pairs)
+    fill_tables(table_ref, width, least)
+    for copy in needed:
         copy.wait()
-    wave, filled = wave_column(waves, held, slots)
-    wave_ref[...] = jnp.broadcast_to(wave, (slots, LANES))
+    choice = slot_choice(waves, held, first, slots)
+    choice_ref[...] = choice
+    widened[...] = given[...].astype(jnp.float32)
+    for c in range(held):
+        for j in range(pairs):
+            strip = widened[c, pl.ds(j, owners, stride=pairs), :]
+            basis_ref[c, j * owners : (j + 1) * owners, :] = turn(strip, -first, 0).astype(
+                jnp.bfloat16
+            )
     lane = lax.broadcasted_iota(jnp.int32, (1, LANES), 1)
+    padding = jnp.zeros((1, LANES - width), jnp.float32)
+    own_waves = jnp.concatenate([waves[...].astype(jnp.float32), padding], axis=1)
+    own_waves = pltpu.roll(own_waves, (LANES - lax.axis_index("lat") * held) % LANES, 1)
+    for c in range(held):
+        wave_ref[c : c + 1, :] = jnp.broadcast_to(own_waves[:, c : c + 1], (1, LANES))
     all_levels = levels.shape[1]
     own = jnp.concatenate([levels[...], jnp.zeros((1, LANES - all_levels), jnp.float32)], axis=1)
     own = pltpu.roll(own, (LANES - lax.axis_index("lev") * fields) % LANES, 1)
     own = jnp.where(lane < fields, own, 0.0)
     stiffness = own
     for copy in range(1, 4):
-        stiffness = stiffness + pltpu.roll(own, copy * fields, 1)
+        stiffness = stiffness + turn(own, copy * fields, 1)
     stiffness_ref[...] = stiffness
-    lane_count = jnp.ones((1, LANES), jnp.float32)
-    for j in range(pairs):
-        lane_count = jnp.where(lane == j, counts[j].astype(jnp.float32), lane_count)
-    lane_inverse = 1.0 / lane_count
-    turn_cos, turn_sin = cos_minus_sin(
-        jnp.broadcast_to(wave * float(LANES), (slots, LANES)), lane_count, lane_inverse
-    )
-    steps = wave * lane.astype(jnp.float32)
-    blocks = table_ref.shape[2] // LANES
     position = lax.broadcasted_iota(jnp.int32, (1, points), 1)
+    real, imaginary, ends, scales = [], [], [], []
     for j in range(pairs):
         count = jnp.full((1, LANES), counts[j].astype(jnp.float32))
         limit_ref[j : j + 1, :] = count
-        inverse = 1.0 / count
-        cosine, sine = cos_minus_sin(steps, count, inverse)
-        kept = filled & (2.0 * wave < count[:, :1])
-        cosine = jnp.where(kept, cosine, 0.0)
-        sine = jnp.where(kept, sine, 0.0)
-        block_cos = turn_cos[:, j : j + 1]
-        block_sin = turn_sin[:, j : j + 1]
-        for block in range(blocks):
-            if block > 0:
-                cosine, sine = (
-                    cosine * block_cos - sine * block_sin,
-                    sine * block_cos + cosine * block_sin,
-                )
-            at = pl.ds(block * LANES, LANES)
-            table_ref[j, :slots, at] = cosine.astype(jnp.bfloat16)
-            table_ref[j, slots:, at] = sine.astype(jnp.bfloat16)
+        ends.append(count)
+        scales.append(jnp.full((1, LANES), weights[j]) / count)
         inside = jnp.where(position < counts[j], 1.0, 0.0).astype(jnp.bfloat16)
         latitude = values[j * rows : (j + 1) * rows, :] * inside
         product = lax.dot_general(
-            table_ref[j, :, :points],
+            table_ref[candidate_of(counts[j], j, least), :, :points],
             latitude,
             (((1,), (1,)), ((), ())),
             preferred_element_type=jnp.float32,
         )
-        product = product * (jnp.full((1, 1), weights[j]) * inverse[:, :1])
-        packed = jnp.concatenate(
-            [
-                product[:slots],
-                product[slots:],
-                jnp.zeros((slots, LANES - 2 * rows), jnp.float32),
-            ],
-            axis=1,
-        )
-        coef_ref[:, j] = packed.reshape(owners, ROWS, LANES).astype(jnp.bfloat16)
-    needed[5].wait()
-
-
-def legendre_kernel(held, fields, wave_ref, stiffness_ref, basis_ref, recv_ref, send_ref, fan_in, fan_out):
-    owners, pairs, _, _ = recv_ref.shape
-    latitudes = owners * pairs
-    width = basis_ref.shape[2]
-    first = lax.axis_index("lat") * ROWS
-    fan_in[...] = recv_ref[...].astype(jnp.float32).reshape(latitudes * ROWS, LANES)
-    stiffness = stiffness_ref[...]
-    lane = lax.broadcasted_iota(jnp.int32, (1, LANES), 1)
-    south = ((lane >= fields) & (lane < 2 * fields)) | (lane >= 3 * fields)
+        real.append(product[:width])
+        imaginary.append(product[width:])
+    end_rows = lane_row(lane, ends, rows)
+    scale_rows = lane_row(lane, scales, rows)
+    mode = lax.broadcasted_iota(jnp.int32, (width, 1), 0).astype(jnp.float32)
+    tail = [jnp.zeros((width, LANES - rest), jnp.float32)] if rest else []
+    for part, pieces in enumerate((real, imaginary)):
+        whole = jnp.concatenate(pieces + tail, axis=1)
+        cut = []
+        for block, (end, scale) in enumerate(zip(end_rows, scale_rows)):
+            strip = whole[:, block * LANES : (block + 1) * LANES]
+            cut.append(jnp.where(2.0 * mode < end, strip * scale, 0.0).astype(jnp.bfloat16))
+        placed = jnp.dot(
+            choice[:, :width], jnp.concatenate(cut, axis=1), preferred_element_type=jnp.float32
+        )
+        cut = [
+            placed[:, block * LANES : (block + 1) * LANES].reshape(owners, ROWS, LANES)
+            for block in range(len(cut))
+        ]
+        if rest:
+            cut[-2] = fold_rest(cut[-2], cut[-1], held, rest)
+        for block in range(blocks):
+            coef_ref[:, block, part] = cut[block].astype(jnp.bfloat16)
+
+
+def legendre_kernel(
+    held, fields, wave_ref, stiffness_ref, basis_ref, recv_ref, send_ref, fan_in, fan_out
+):
+    owners, blocks = recv_ref.shape[:2]
+    latitudes, width = basis_ref.shape[1:]
+    pairs = latitudes // owners
+    rows = 2 * fields
+    rest = pairs * rows - blocks * LANES
+    chunk = blocks * 2 * ROWS
+    fan_in[...] = recv_ref[...].astype(jnp.float32).reshape(owners * chunk, LANES)
+
+    def chunk_rows(block, part, row):
+        return pl.ds((block * 2 + part) * ROWS + row, owners, stride=chunk)
+
+    def home(c, block, lane):
+        if block == blocks:
+            row, start = rest_home(c, held, rest)
+            return row, block - 1, start + lane
+        return c, block, lane
+
+    lane_at = lax.broadcasted_iota(jnp.int32, (1, LANES), 1)
+    south = ((lane_at >= fields) & (lane_at < 2 * fields)) | (lane_at >= 3 * fields)
     offset = lax.broadcasted_iota(jnp.int32, (width, 1), 0)
     parity = jnp.where((offset & 1) == 0, 1.0, -1.0)
     offset = offset.astype(jnp.float32)
+    empty = jnp.zeros((owners, LANES), jnp.float32)
+    folded = {}
     for c in range(held):
-        wave = wave_ref[pl.ds(first + c, 1), :]
+        wave = wave_ref[c : c + 1, :]
         degree = offset + wave
-        factor = 1.0 / (1.0 + stiffness * degree * (degree + 1.0))
+        basis = basis_ref[c]
+        strips = []
+        for j in range(pairs):
+            strip = empty
+            for part in range(2):
+                for block, lane, place, size in segments(j * rows, rows):
+                    row, block, lane = home(c, block, lane)
+                    source = fan_in[chunk_rows(block, part, row), :]
+                    target = part * rows + place
+                    here = (lane_at >= target) & (lane_at < target + size)
+                    strip = jnp.where(here, turn(source, target - lane, 1), strip)
+            strips.append(strip.astype(jnp.bfloat16))
+        spectra = lax.dot_general(
+            basis,
+            jnp.concatenate(strips, axis=0),
+            (((0,), (0,)), ((), ())),
+            preferred_element_type=jnp.float32,
+        )
+        factor = 1.0 / (1.0 + stiffness_ref[...] * degree * (degree + 1.0))
         damping = jnp.where(degree < float(width), factor, 0.0)
-        block = fan_in[pl.ds(c, latitudes, stride=ROWS), :].astype(jnp.bfloat16)
-        basis = basis_ref[c]
-        spectra = lax.dot_general(
-            basis, block, (((0,), (0,)), ((), ())), preferred_element_type=jnp.float32
-        )
-        other = jnp.where(
-            south, pltpu.roll(spectra, fields, 1), pltpu.roll(spectra, LANES - fields, 1)
-        )
+        other = jnp.where(south, turn(spectra, fields, 1), turn(spectra, -fields, 1))
         scaled = ((spectra + parity * other) * damping).astype(jnp.bfloat16)
         returned = jnp.dot(basis, scaled, preferred_element_type=jnp.float32)
         returned = returned * jnp.where(wave == 0.0, 1.0, 2.0)
-        fan_out[pl.ds(c, latitudes, stride=ROWS), :] = returned
-    for c in range(held, ROWS):
-        fan_out[pl.ds(c, latitudes, stride=ROWS), :] = jnp.zeros((latitudes, LANES), jnp.float32)
-    send_ref[...] = fan_out[...].reshape(owners, pairs, ROWS, LANES).astype(jnp.bfloat16)
-
-
-def synthesis_kernel(limit_ref, recv_ref, table_ref, grid_hbm, values, left):
-    owners, pairs, _, _ = recv_ref.shape
+        for part in range(2):
+            built = {}
+            for j in range(pairs):
+                strip = returned[j * owners : (j + 1) * owners]
+                for block, lane, place, size in segments(j * rows, rows):
+                    row, block, lane = home(c, block, lane)
+                    key = (block, part, row)
+                    here = (lane_at >= lane) & (lane_at < lane + size)
+                    moved = turn(strip, lane - part * rows - place, 1)
+                    held_in = folded if row >= held else built
+                    held_in[key] = jnp.where(here, moved, held_in.get(key, empty))
+            for key, value in built.items():
+                fan_out[chunk_rows(*key), :] = value
+    for block in range(blocks):
+        for part in range(2):
+            for row in range(held, ROWS):
+                key = (block, part, row)
+                fan_out[chunk_rows(*key), :] = folded.get(key, empty)
+    send_ref[...] = fan_out[...].astype(jnp.bfloat16).reshape(send_ref.shape)
+
+
+def synthesis_kernel(
+    held, limit_ref, choice_ref, recv_ref, table_ref, grid_hbm, values, left
+):
+    owners, blocks = recv_ref.shape[:2]
+    pairs = limit_ref.shape[0]
     slots = owners * ROWS
+    width = table_ref.shape[1] // 2
     points = grid_hbm.shape[1]
     rows = grid_hbm.shape[0] // pairs
+    rest = pairs * rows - blocks * LANES
+    least = least_count(pairs)
+    choice = choice_ref[...]
+    operands = []
+    for part in range(2):
+        cut = [recv_ref[:, block, part].astype(jnp.float32) for block in range(blocks)]
+        if rest:
+            cut.append(unfold_rest(cut[-1], held, rest))
+        across = jnp.concatenate([strip.reshape(slots, LANES).T for strip in cut], axis=0)
+        operands.append(
+            jnp.dot(
+                across[: pairs * rows].astype(jnp.bfloat16),
+                choice,
+                preferred_element_type=jnp.float32,
+            )
+        )
     position = lax.broadcasted_iota(jnp.int32, (1, points), 1).astype(jnp.float32)
+    mode = lax.broadcasted_iota(jnp.int32, (1, LANES), 1).astype(jnp.float32)
     copies = []
     for j in range(pairs):
-        block = recv_ref[:, j].astype(jnp.float32).reshape(slots, LANES)
-        operand = jnp.concatenate([block[:, :rows], block[:, rows : 2 * rows]], axis=0)
-        product = lax.dot_general(
-            operand.astype(jnp.bfloat16),
-            table_ref[j],
-            (((0,), (0,)), ((), ())),
-            preferred_element_type=jnp.float32,
-        )
-        kept = jnp.where(position < limit_ref[j : j + 1, :1], product[:, :points], 0.0)
+        end = limit_ref[j : j + 1, :]
         at = pl.ds(j * rows, rows)
+        candidate = candidate_of(jnp.max(end).astype(jnp.int32), j, least)
+        product = None
+        for part in range(2):
+            operand = operands[part][j * rows : (j + 1) * rows]
+            operand = jnp.where(2.0 * mode < end, operand, 0.0).astype(jnp.bfloat16)
+            term = jnp.dot(
+                operand[:, :width],
+                table_ref[candidate, part * width : (part + 1) * width, :],
+                preferred_element_type=jnp.float32,
+            )
+            product = term if product is None else product + term
+        kept = jnp.where(position < end[:, :1], product[:, :points], 0.0)
         values[at, :] = kept.astype(jnp.bfloat16)
         copies.append(pltpu.make_async_copy(values.at[at, :], grid_hbm.at[at, :], left.at[j]))
         copies[-1].start()
@@ -192,36 +352,43 @@
         copy.wait()
 
 
-def on_device(grid, point_counts, waves, legendre, weights, stiffness):
+def on_device(mesh, grid, point_counts, waves, legendre, weights, stiffness):
     pairs, _, fields, points = grid.shape
-    held = legendre.shape[0]
     width = waves.shape[0]
-    owners = width // held
+    owners = mesh.shape["lat"]
+    held = width // owners
     slots = owners * ROWS
     rows = 2 * fields
     padded = -(-points // LANES) * LANES
+    blocks = pairs * rows // LANES
+    chunk = blocks * 2 * ROWS
+    first = 5 * owners // 8
+    groups = [[(place + first) % owners for place in range(owners)]]
     vmem = pl.BlockSpec(memory_space=pltpu.VMEM)
     hbm = pl.BlockSpec(memory_space=pltpu.HBM)
     limits = pltpu.CompilerParams(vmem_limit_bytes=KERNEL_BYTES)
-    exchanged = jax.ShapeDtypeStruct((owners, pairs, ROWS, LANES), jnp.bfloat16)
-    coefficients, tables, basis, wave_rows, levels, ends = pl.pallas_call(
-        functools.partial(analysis_kernel, held, fields),
+    exchanged = jax.ShapeDtypeStruct((owners, blocks, 2, ROWS, LANES), jnp.bfloat16)
+    coefficients, tables, choice, basis, wave_rows, levels, ends = pl.pallas_call(
+        functools.partial(analysis_kernel, held, fields, first),
         out_shape=(
             exchanged,
-            jax.ShapeDtypeStruct((pairs, 2 * slots, padded), jnp.bfloat16),
-            jax.ShapeDtypeStruct(legendre.shape, legendre.dtype),
-            jax.ShapeDtypeStruct((slots, LANES), jnp.float32),
+            jax.ShapeDtypeStruct((pairs + 1, 2 * width, padded), jnp.bfloat16),
+            jax.ShapeDtypeStruct((slots, LANES), jnp.bfloat16),
+            jax.ShapeDtypeStruct(legendre.shape, jnp.bfloat16),
+            jax.ShapeDtypeStruct((held, LANES), jnp.float32),
             jax.ShapeDtypeStruct((1, LANES), jnp.float32),
             jax.ShapeDtypeStruct((pairs, LANES), jnp.float32),
         ),
         in_specs=[hbm] * 6,
-        out_specs=(vmem,) * 6,
+        out_specs=(vmem,) * 7,
         scratch_shapes=[
             pltpu.SMEM((pairs,), jnp.int32),
             pltpu.SMEM((pairs,), jnp.float32),
             pltpu.VMEM((1, width), jnp.int32),
             pltpu.VMEM((1, stiffness.shape[0]), jnp.float32),
             pltpu.VMEM((pairs * rows, points), jnp.bfloat16),
+            pltpu.VMEM(legendre.shape, jnp.bfloat16),
+            pltpu.VMEM(legendre.shape, jnp.float32),
             pltpu.SemaphoreType.DMA((6,)),
         ],
         compiler_params=limits,
@@ -235,24 +402,28 @@
             )
         )
     )
-    received = lax.all_to_all(coefficients, "lat", split_axis=0, concat_axis=0, tiled=True)
+
+    def exchange(array):
+        return lax.all_to_all(
+            array, "lat", split_axis=0, concat_axis=0, axis_index_groups=groups, tiled=True
+        )
+
     synthesised = pl.pallas_call(
         functools.partial(legendre_kernel, held, fields),
         out_shape=exchanged,
         in_specs=[vmem] * 4,
         out_specs=vmem,
         scratch_shapes=[
-            pltpu.VMEM((owners * pairs * ROWS, LANES), jnp.float32),
-            pltpu.VMEM((owners * pairs * ROWS, LANES), jnp.float32),
+            pltpu.VMEM((owners * chunk, LANES), jnp.float32),
+            pltpu.VMEM((owners * chunk, LANES), jnp.float32),
         ],
         compiler_params=limits,
         name="legendre",
-    )(wave_rows, levels, basis, received)
-    returned = lax.all_to_all(synthesised, "lat", split_axis=0, concat_axis=0, tiled=True)
+    )(wave_rows, levels, basis, exchange(coefficients))
     result = pl.pallas_call(
-        synthesis_kernel,
+        functools.partial(synthesis_kernel, held),
         out_shape=jax.ShapeDtypeStruct((pairs * rows, points), jnp.bfloat16),
-        in_specs=[vmem] * 3,
+        in_specs=[vmem] * 4,
         out_specs=hbm,
         scratch_shapes=[
             pltpu.VMEM((pairs * rows, points), jnp.bfloat16),
@@ -260,7 +431,7 @@
         ],
         compiler_params=limits,
         name="synthesis",
-    )(ends, returned, tables)
+    )(ends, choice, exchange(synthesised), tables)
     return result.reshape(grid.shape)
 
 
@@ -375,16 +546,25 @@
     return lax.map(synthesise, (returned, matrices, twist_cos, twist_sin, point_counts))
 
 
-def fits_on_chip(mesh, grid, legendre, stiffness):
-    owners, levels = mesh.shape["lat"], mesh.shape["lev"]
-    pairs, fields = grid.shape[0] // owners, grid.shape[2] // levels
-    held = legendre.shape[0] // owners
-    table_bytes = 4 * pairs * owners * ROWS * grid.shape[3]
+def fits_on_chip(mesh, grid, waves, stiffness):
+    owners = mesh.shape["lat"]
+    pairs, fields = grid.shape[0] // owners, grid.shape[2] // mesh.shape["lev"]
+    width, points = waves.shape[0], grid.shape[3]
+    held = width // owners
+    lanes = 2 * pairs * fields
+    rest = lanes % LANES
     return (
-        table_bytes <= TABLE_BUDGET
+        width % owners == 0
+        and width % (2 * ROWS) == 0
+        and width <= LANES
+        and 4 * (pairs + 1) * width * points <= TABLE_BUDGET
+        and points <= ROWS * LANES
         and held <= ROWS
+        and lanes >= LANES
+        and (rest == 0 or held * rest <= (ROWS - held) * (LANES - LANES % rest))
         and 4 * fields <= LANES
         and fields % ROWS == 0
+        and owners % (2 * ROWS) == 0
         and stiffness.shape[0] <= LANES
     )
 
@@ -394,7 +574,8 @@
     out_specs = P("lat", None, "lev", None)
 
     def program(grid, point_counts, waves, legendre, weights, stiffness):
-        body = on_device if fits_on_chip(mesh, grid, legendre, stiffness) else on_device_blocked
+        fits = fits_on_chip(mesh, grid, waves, stiffness)
+        body = functools.partial(on_device, mesh) if fits else on_device_blocked
         return jax.shard_map(
             body, mesh=mesh, in_specs=in_specs, out_specs=out_specs, check_vma=False
         )(grid, point_counts, waves, legendre, weights, stiffness)

time: 32.7 us -> 27.7 us (0.85)
  blocking collectives: 28.1 us -> 23.4 us
    all_to_all x2, blocking collectives: 28.1 us -> 23.4 us  [exchange(): lax.all_to_all(array, 'lat', split_axis=0, concat_axis=0, axis_index_grou...]
    pallas_call x2, Pallas kernels: 3.82 us -> 3.22 us  [the longest x1 1.94 us: on_device(): pl.pallas_call(functools.partial(analysis_kernel, held, fields, first), o...]
where the time goes in v4:
time: 27.7 us; the launch traced here: 27.5 us
  blocking collectives  23.4 us (84%)
  Pallas kernels  4.06 us (15%)
    all_to_all x2, blocking collectives, exchange(): lax.all_to_all(array, 'lat', split_axis=0, concat_axis=0, axis_index_grou...  23.4 us
    pallas_call x1, Pallas kernels, on_device(): pl.pallas_call(functools.partial(analysis_kernel, held, fields, first), o...  1.94 us
    pallas_call x1, Pallas kernels, on_device(): pl.pallas_call(functools.partial(synthesis_kernel, held), out_shape=jax.S...  1.28 us
    pallas_call x1, Pallas kernels, on_device(): pl.pallas_call(functools.partial(legendre_kernel, held, fields), out_shap...  0.84 us

profile of v4, /device:TPU:0, one launch (start us, length us, event | category | flops | bytes accessed | tf_op | source)
XLA Modules:
  0.0 27.5 jit_solution(5379871803135068115)
XLA Ops:
  0.0 1.9 %analysis.1 = (bf16[16,2,2,8,128]{4,3,2,1,0:T(8,128)(2,1)S(1)}, bf16[7,192,512]{2,1,0:T(8,128)(2,1)S(1)}, bf16[128,128]{1,0:T(8,128)(2,1)S(1)}, bf16[6,96,96]{2,...) custom-call(s32[6]{0:T(128)} %counts_hbm.1, f32[6]{0:T(128)} %weights_hbm.1, ...), custom_call_target="tpu_custom_call" | custom-call | tf_op jit(solution)/shard_map/analysis/pallas_call | solution.py:371
  2.0 13.3 %all_to_all.10.recv_ref = bf16[16,2,2,8,128]{4,3,2,1,0:T(8,128)(2,1)S(1)} all-to-all(bf16[16,2,2,8,128]{4,3,2,1,0:T(8,128)(2,1)S(1)} %get-tuple-element.17), channel_id=1, replica_groups={{20,22,24,26,28,30,0,2,4,6,8,10,12,14,16,18},{21,23,25,27,29,31,1,3,5,7..., dimensions={0} | all-to-all | bytes 262144 | tf_op jit(solution)/shard_map/all_to_all | solution.py:407
  15.3 0.8 %legendre.1 = bf16[16,2,2,8,128]{4,3,2,1,0:T(8,128)(2,1)S(1)} custom-call(f32[6,128]{1,0:T(8,128)S(1)} %get-tuple-element.14.wave_ref, f32[1,128]{1,0:T(1,128)S(1)} %get-tuple-element.15.stiffness_ref, bf16[6,96,96]{2,1,0:T(8,128)(2,1)S(1)} %get-tuple-element.16.basis_ref, bf16[16,2,2,8,128]{4,3,2,1,0:T(8,128)(2,1)S(1)} %all_to_all.10.recv_ref), custom_call_target="tpu_custom_call" | custom-call | tf_op jit(solution)/shard_map/legendre/pallas_call | solution.py:411
  16.1 10.1 %all_to_all.11.recv_ref = bf16[16,2,2,8,128]{4,3,2,1,0:T(8,128)(2,1)S(1)} all-to-all(bf16[16,2,2,8,128]{4,3,2,1,0:T(8,128)(2,1)S(1)} %legendre.1), channel_id=1, replica_groups={{20,22,24,26,28,30,0,2,4,6,8,10,12,14,16,18},{21,23,25,27,29,31,1,3,5,7..., dimensions={0} | all-to-all | bytes 262144 | tf_op jit(solution)/shard_map/all_to_all | solution.py:407
  26.2 1.3 %synthesis.1 = bf16[288,400]{1,0:T(8,128)(2,1)} custom-call(f32[6,128]{1,0:T(8,128)S(1)} %get-tuple-element.12.limit_ref, bf16[128,128]{1,0:T(8,128)(2,1)S(1)} %get-tuple-element.13.choice_ref, bf16[16,2,2,8,128]{4,3,2,1,0:T(8,128)(2,1)S(1)} %all_to_all.11.recv_ref, bf16[7,192,512]{2,1,0:T(8,128)(2,1)S(1)} %get-tuple-element.18.table_ref), custom_call_target="tpu_custom_call" | custom-call | tf_op jit(solution)/shard_map/synthesis/pallas_call | solution.py:423

commit v5 on v4

--- a/solution.py
+++ b/solution.py
@@ -51,7 +51,7 @@
     waves = jnp.broadcast_to(waves_ref[...].astype(jnp.float32) + 1.0, (slots, width))
     column = jnp.sum(jnp.where(chosen, waves, 0.0), axis=1, keepdims=True)
     mode = lax.broadcasted_iota(jnp.int32, (slots, LANES), 1).astype(jnp.float32) + 1.0
-    return jnp.where(mode == column, 1.0, 0.0).astype(jnp.bfloat16)
+    return jnp.where(mode == column, 1.0, 0.0)
 
 
 def segments(start, length):
@@ -85,24 +85,19 @@
     return held + c // fit, (c % fit) * rest
 
 
-def fold_rest(whole, part, held, rest):
+def rest_choices(choice, held, rest):
+    owners = choice.shape[0] // ROWS
+    grouped = choice.reshape(owners, ROWS, LANES)
     sublane = lax.broadcasted_iota(jnp.int32, (1, ROWS, LANES), 1)
-    lane = lax.broadcasted_iota(jnp.int32, (1, ROWS, LANES), 2)
-    for c in range(held):
-        row, start = rest_home(c, held, rest)
-        moved = turn(turn(part, row - c, 1), start, 2)
-        here = (sublane == row) & (lane >= start) & (lane < start + rest)
-        whole = jnp.where(here, moved, whole)
-    return whole
-
-
-def unfold_rest(whole, held, rest):
-    sublane = lax.broadcasted_iota(jnp.int32, (1, ROWS, LANES), 1)
-    part = whole
-    for c in range(held):
-        row, start = rest_home(c, held, rest)
-        part = jnp.where(sublane == c, turn(turn(whole, c - row, 1), -start, 2), part)
-    return part
+    fit = LANES // rest
+    out = []
+    for group in range(min(fit, held)):
+        total = jnp.zeros_like(grouped)
+        for c in range(group, held, fit):
+            row, _ = rest_home(c, held, rest)
+            total = jnp.where(sublane == row, turn(grouped, row - c, 1), total)
+        out.append(total.reshape(choice.shape))
+    return out
 
 
 def fill_tables(table_ref, width, least):
@@ -142,7 +137,7 @@
     held, fields, first,
     counts_hbm, weights_hbm, waves_hbm, stiffness_hbm, basis_hbm, grid_hbm,
     coef_ref, table_ref, choice_ref, basis_ref, wave_ref, stiffness_ref, limit_ref,
-    counts, weights, waves, levels, values, given, widened, arrived,
+    counts, weights, waves, levels, values, given, widened, arrived, grid_arrived,
 ):
     owners, blocks = coef_ref.shape[:2]
     pairs = limit_ref.shape[0]
@@ -151,21 +146,26 @@
     points = grid_hbm.shape[1]
     rows = grid_hbm.shape[0] // pairs
     rest = pairs * rows - blocks * LANES
-    needed = [
+    small = [
         pltpu.make_async_copy(source, target, arrived.at[k])
         for k, (source, target) in enumerate(
-            [(counts_hbm, counts), (waves_hbm, waves), (weights_hbm, weights),
-             (stiffness_hbm, levels), (grid_hbm, values), (basis_hbm, given)]
+            [(counts_hbm, counts), (waves_hbm, waves), (weights_hbm, weights), (stiffness_hbm, levels)]
         )
     ]
-    for copy in needed:
+    latitudes = [pl.ds(j * rows, rows) for j in range(pairs)]
+    fields_in = [pltpu.make_async_copy(grid_hbm, values, grid_arrived)]
+    basis_in = pltpu.make_async_copy(basis_hbm, given, arrived.at[len(small)])
+    for copy in (*fields_in, *small, basis_in):
         copy.start()
     least = least_count(pairs)
     fill_tables(table_ref, width, least)
-    for copy in needed:
+    for copy in (*small, *fields_in, basis_in):
         copy.wait()
     choice = slot_choice(waves, held, first, slots)
-    choice_ref[...] = choice
+    choices = [choice] + (rest_choices(choice, held, rest) if rest else [])
+    choices = [each.astype(jnp.bfloat16) for each in choices]
+    for k, each in enumerate(choices):
+        choice_ref[k * slots : (k + 1) * slots, :] = each
     widened[...] = given[...].astype(jnp.float32)
     for c in range(held):
         for j in range(pairs):
@@ -194,37 +194,43 @@
         limit_ref[j : j + 1, :] = count
         ends.append(count)
         scales.append(jnp.full((1, LANES), weights[j]) / count)
+    end_rows = lane_row(lane, ends, rows)
+    scale_rows = lane_row(lane, scales, rows)
+    for j in range(pairs):
         inside = jnp.where(position < counts[j], 1.0, 0.0).astype(jnp.bfloat16)
-        latitude = values[j * rows : (j + 1) * rows, :] * inside
         product = lax.dot_general(
             table_ref[candidate_of(counts[j], j, least), :, :points],
-            latitude,
+            values[latitudes[j], :] * inside,
             (((1,), (1,)), ((), ())),
             preferred_element_type=jnp.float32,
         )
         real.append(product[:width])
         imaginary.append(product[width:])
-    end_rows = lane_row(lane, ends, rows)
-    scale_rows = lane_row(lane, scales, rows)
     mode = lax.broadcasted_iota(jnp.int32, (width, 1), 0).astype(jnp.float32)
     tail = [jnp.zeros((width, LANES - rest), jnp.float32)] if rest else []
-    for part, pieces in enumerate((real, imaginary)):
+    cut = [[] for _ in end_rows]
+    for pieces in (real, imaginary):
         whole = jnp.concatenate(pieces + tail, axis=1)
-        cut = []
         for block, (end, scale) in enumerate(zip(end_rows, scale_rows)):
             strip = whole[:, block * LANES : (block + 1) * LANES]
-            cut.append(jnp.where(2.0 * mode < end, strip * scale, 0.0).astype(jnp.bfloat16))
+            cut[block].append(jnp.where(2.0 * mode < end, strip * scale, 0.0))
+    cut = [jnp.concatenate(both, axis=1) for both in cut]
+    unread = jnp.zeros((LANES - width, 2 * LANES), jnp.bfloat16)
+    for block in range(blocks):
+        taken, modes = [choices[0]], [cut[block].astype(jnp.bfloat16), unread]
+        if rest and block == blocks - 1:
+            for group, each in enumerate(choices[1:]):
+                moved = [turn(cut[-1][:, k * LANES : (k + 1) * LANES], group * rest, 1) for k in range(2)]
+                taken.append(each)
+                modes += [jnp.concatenate(moved, axis=1).astype(jnp.bfloat16), unread]
         placed = jnp.dot(
-            choice[:, :width], jnp.concatenate(cut, axis=1), preferred_element_type=jnp.float32
-        )
-        cut = [
-            placed[:, block * LANES : (block + 1) * LANES].reshape(owners, ROWS, LANES)
-            for block in range(len(cut))
-        ]
-        if rest:
-            cut[-2] = fold_rest(cut[-2], cut[-1], held, rest)
-        for block in range(blocks):
-            coef_ref[:, block, part] = cut[block].astype(jnp.bfloat16)
+            jnp.concatenate(taken, axis=1),
+            jnp.concatenate(modes, axis=0),
+            preferred_element_type=jnp.float32,
+        )
+        for part in range(2):
+            strip = placed[:, part * LANES : (part + 1) * LANES]
+            coef_ref[:, block, part] = strip.reshape(owners, ROWS, LANES).astype(jnp.bfloat16)
 
 
 def legendre_kernel(
@@ -235,11 +241,13 @@
     pairs = latitudes // owners
     rows = 2 * fields
     rest = pairs * rows - blocks * LANES
-    chunk = blocks * 2 * ROWS
-    fan_in[...] = recv_ref[...].astype(jnp.float32).reshape(owners * chunk, LANES)
+    for block in range(blocks):
+        for part in range(2):
+            plane = recv_ref[:, block, part].astype(jnp.float32).reshape(owners * ROWS, LANES)
+            fan_in[block * 2 + part] = plane
 
     def chunk_rows(block, part, row):
-        return pl.ds((block * 2 + part) * ROWS + row, owners, stride=chunk)
+        return block * 2 + part, pl.ds(row, owners, stride=ROWS), slice(None)
 
     def home(c, block, lane):
         if block == blocks:
@@ -264,7 +272,7 @@
             for part in range(2):
                 for block, lane, place, size in segments(j * rows, rows):
                     row, block, lane = home(c, block, lane)
-                    source = fan_in[chunk_rows(block, part, row), :]
+                    source = fan_in[chunk_rows(block, part, row)]
                     target = part * rows + place
                     here = (lane_at >= target) & (lane_at < target + size)
                     strip = jnp.where(here, turn(source, target - lane, 1), strip)
@@ -293,13 +301,16 @@
                     held_in = folded if row >= held else built
                     held_in[key] = jnp.where(here, moved, held_in.get(key, empty))
             for key, value in built.items():
-                fan_out[chunk_rows(*key), :] = value
+                fan_out[chunk_rows(*key)] = value
     for block in range(blocks):
         for part in range(2):
             for row in range(held, ROWS):
                 key = (block, part, row)
-                fan_out[chunk_rows(*key), :] = folded.get(key, empty)
-    send_ref[...] = fan_out[...].astype(jnp.bfloat16).reshape(send_ref.shape)
+                fan_out[chunk_rows(*key)] = folded.get(key, empty)
+    for block in range(blocks):
+        for part in range(2):
+            plane = fan_out[block * 2 + part].reshape(owners, ROWS, LANES)
+            send_ref[:, block, part] = plane.astype(jnp.bfloat16)
 
 
 def synthesis_kernel(
@@ -313,20 +324,30 @@
     rows = grid_hbm.shape[0] // pairs
     rest = pairs * rows - blocks * LANES
     least = least_count(pairs)
-    choice = choice_ref[...]
     operands = []
     for part in range(2):
-        cut = [recv_ref[:, block, part].astype(jnp.float32) for block in range(blocks)]
-        if rest:
-            cut.append(unfold_rest(cut[-1], held, rest))
-        across = jnp.concatenate([strip.reshape(slots, LANES).T for strip in cut], axis=0)
-        operands.append(
+        turned = []
+        for block in range(blocks):
+            plane = recv_ref[:, block, part].astype(jnp.float32).reshape(slots, LANES)
+            turned.append(plane.T.astype(jnp.bfloat16))
+        found = [
             jnp.dot(
-                across[: pairs * rows].astype(jnp.bfloat16),
-                choice,
+                jnp.concatenate(turned, axis=0),
+                choice_ref[:slots, :],
                 preferred_element_type=jnp.float32,
             )
-        )
+        ]
+        if rest:
+            groups = choice_ref.shape[0] // slots - 1
+            folded = [turned[-1][group * rest : (group + 1) * rest] for group in range(groups)]
+            found.append(
+                jnp.dot(
+                    jnp.concatenate(folded, axis=1),
+                    choice_ref[slots:, :],
+                    preferred_element_type=jnp.float32,
+                )
+            )
+        operands.append(jnp.concatenate(found, axis=0))
     position = lax.broadcasted_iota(jnp.int32, (1, points), 1).astype(jnp.float32)
     mode = lax.broadcasted_iota(jnp.int32, (1, LANES), 1).astype(jnp.float32)
     copies = []
@@ -361,7 +382,8 @@
     rows = 2 * fields
     padded = -(-points // LANES) * LANES
     blocks = pairs * rows // LANES
-    chunk = blocks * 2 * ROWS
+    rest = pairs * rows % LANES
+    choices = 1 + (min(LANES // rest, held) if rest else 0)
     first = 5 * owners // 8
     groups = [[(place + first) % owners for place in range(owners)]]
     vmem = pl.BlockSpec(memory_space=pltpu.VMEM)
@@ -373,7 +395,7 @@
         out_shape=(
             exchanged,
             jax.ShapeDtypeStruct((pairs + 1, 2 * width, padded), jnp.bfloat16),
-            jax.ShapeDtypeStruct((slots, LANES), jnp.bfloat16),
+            jax.ShapeDtypeStruct((choices * slots, LANES), jnp.bfloat16),
             jax.ShapeDtypeStruct(legendre.shape, jnp.bfloat16),
             jax.ShapeDtypeStruct((held, LANES), jnp.float32),
             jax.ShapeDtypeStruct((1, LANES), jnp.float32),
@@ -389,7 +411,8 @@
             pltpu.VMEM((pairs * rows, points), jnp.bfloat16),
             pltpu.VMEM(legendre.shape, jnp.bfloat16),
             pltpu.VMEM(legendre.shape, jnp.float32),
-            pltpu.SemaphoreType.DMA((6,)),
+            pltpu.SemaphoreType.DMA((5,)),
+            pltpu.SemaphoreType.DMA,
         ],
         compiler_params=limits,
         name="analysis",
@@ -414,8 +437,8 @@
         in_specs=[vmem] * 4,
         out_specs=vmem,
         scratch_shapes=[
-            pltpu.VMEM((owners * chunk, LANES), jnp.float32),
-            pltpu.VMEM((owners * chunk, LANES), jnp.float32),
+            pltpu.VMEM((blocks * 2, slots, LANES), jnp.float32),
+            pltpu.VMEM((blocks * 2, slots, LANES), jnp.float32),
         ],
         compiler_params=limits,
         name="legendre",
@@ -561,7 +584,8 @@
         and points <= ROWS * LANES
         and held <= ROWS
         and lanes >= LANES
-        and (rest == 0 or held * rest <= (ROWS - held) * (LANES - LANES % rest))
+        and (rest == 0 or rest % (2 * ROWS) == 0)
+        and (rest == 0 or held <= (ROWS - held) * (LANES // rest))
         and 4 * fields <= LANES
         and fields % ROWS == 0
         and owners % (2 * ROWS) == 0

time: 27.7 us -> 27.5 us (level)
  no operation moved by 1% of the time
where the time goes in v5:
time: 27.5 us; the launch traced here: 27.3 us
  blocking collectives  23.4 us (85%)
  Pallas kernels  3.92 us (14%)
    all_to_all x2, blocking collectives, exchange(): lax.all_to_all(array, 'lat', split_axis=0, concat_axis=0, axis_index_grou...  23.4 us
    pallas_call x1, Pallas kernels, on_device(): pl.pallas_call(functools.partial(analysis_kernel, held, fields, first), o...  1.95 us
    pallas_call x1, Pallas kernels, on_device(): pl.pallas_call(functools.partial(synthesis_kernel, held), out_shape=jax.S...  1.25 us
    pallas_call x1, Pallas kernels, on_device(): pl.pallas_call(functools.partial(legendre_kernel, held, fields), out_shap...  0.72 us

profile of v5, /device:TPU:0, one launch (start us, length us, event | category | flops | bytes accessed | tf_op | source)
XLA Modules:
  0.0 27.3 jit_solution(16035490118967258302)
XLA Ops:
  0.0 1.9 %analysis.1 = (bf16[16,2,2,8,128]{4,3,2,1,0:T(8,128)(2,1)S(1)}, bf16[7,192,512]{2,1,0:T(8,128)(2,1)S(1)}, bf16[640,128]{1,0:T(8,128)(2,1)S(1)}, bf16[6,96,96]{2,...) custom-call(s32[6]{0:T(128)} %counts_hbm.1, f32[6]{0:T(128)} %weights_hbm.1, ...), custom_call_target="tpu_custom_call" | custom-call | tf_op jit(solution)/shard_map/analysis/pallas_call | solution.py:393
  2.0 13.3 %all_to_all.10.recv_ref = bf16[16,2,2,8,128]{4,3,2,1,0:T(8,128)(2,1)S(1)} all-to-all(bf16[16,2,2,8,128]{4,3,2,1,0:T(8,128)(2,1)S(1)} %get-tuple-element.17), channel_id=1, replica_groups={{20,22,24,26,28,30,0,2,4,6,8,10,12,14,16,18},{21,23,25,27,29,31,1,3,5,7..., dimensions={0} | all-to-all | bytes 262144 | tf_op jit(solution)/shard_map/all_to_all | solution.py:430
  15.3 0.7 %legendre.1 = bf16[16,2,2,8,128]{4,3,2,1,0:T(8,128)(2,1)S(1)} custom-call(f32[6,128]{1,0:T(8,128)S(1)} %get-tuple-element.14.wave_ref, f32[1,128]{1,0:T(1,128)S(1)} %get-tuple-element.15.stiffness_ref, bf16[6,96,96]{2,1,0:T(8,128)(2,1)S(1)} %get-tuple-element.16.basis_ref, bf16[16,2,2,8,128]{4,3,2,1,0:T(8,128)(2,1)S(1)} %all_to_all.10.recv_ref), custom_call_target="tpu_custom_call" | custom-call | tf_op jit(solution)/shard_map/legendre/pallas_call | solution.py:434
  16.0 10.1 %all_to_all.11.recv_ref = bf16[16,2,2,8,128]{4,3,2,1,0:T(8,128)(2,1)S(1)} all-to-all(bf16[16,2,2,8,128]{4,3,2,1,0:T(8,128)(2,1)S(1)} %legendre.1), channel_id=1, replica_groups={{20,22,24,26,28,30,0,2,4,6,8,10,12,14,16,18},{21,23,25,27,29,31,1,3,5,7..., dimensions={0} | all-to-all | bytes 262144 | tf_op jit(solution)/shard_map/all_to_all | solution.py:430
  26.1 1.3 %synthesis.1 = bf16[288,400]{1,0:T(8,128)(2,1)} custom-call(f32[6,128]{1,0:T(8,128)S(1)} %get-tuple-element.12.limit_ref, bf16[640,128]{1,0:T(8,128)(2,1)S(1)} %get-tuple-element.13.choice_ref, bf16[16,2,2,8,128]{4,3,2,1,0:T(8,128)(2,1)S(1)} %all_to_all.11.recv_ref, bf16[7,192,512]{2,1,0:T(8,128)(2,1)S(1)} %get-tuple-element.18.table_ref), custom_call_target="tpu_custom_call" | custom-call | tf_op jit(solution)/shard_map/synthesis/pallas_call | solution.py:446

commit v6 on v5

--- a/solution.py
+++ b/solution.py
@@ -66,18 +66,6 @@
 def turn(x, shift, axis):
     shift %= x.shape[axis]
     return pltpu.roll(x, shift, axis) if shift else x
-
-
-def lane_row(lane, pieces, rows):
-    out = []
-    for block in range(-(-len(pieces) * rows // LANES)):
-        total = jnp.zeros((1, LANES), jnp.float32)
-        for j, piece in enumerate(pieces):
-            start, stop = j * rows - block * LANES, (j + 1) * rows - block * LANES
-            if start < LANES and stop > 0:
-                total = jnp.where((lane >= start) & (lane < stop), piece, total)
-        out.append(total)
-    return out
 
 
 def rest_home(c, held, rest):
@@ -121,8 +109,33 @@
                 cosines.append(twice * cosines[-1] - cosines[-2])
                 sines.append(twice * sines[-1] - sines[-2])
             at = pl.ds(b * LANES, LANES)
-            table_ref[i, :width, at] = jnp.concatenate(cosines, axis=0).astype(jnp.bfloat16)
-            table_ref[i, width:, at] = jnp.concatenate(sines, axis=0).astype(jnp.bfloat16)
+            for part, values in enumerate((cosines, sines)):
+                rows = pl.ds(part * width, width)
+                table_ref[i, rows, at] = jnp.concatenate(values, axis=0).astype(jnp.bfloat16)
+
+
+def fill_turned(turned_ref, least):
+    candidates, points, _ = turned_ref.shape
+    sublane = lax.broadcasted_iota(jnp.int32, (ROWS, LANES), 0)
+    lane = lax.broadcasted_iota(jnp.int32, (ROWS, LANES), 1)
+    strides = (ROWS * lane).astype(jnp.float32)
+    for i in range(candidates):
+        count = jnp.full((1, LANES), (least + 4 * i).astype(jnp.float32))
+        inverse = 1.0 / count
+        turn_cos, turn_sin = cos_minus_sin(strides, count, inverse)
+        twice = turn_cos + turn_cos
+        for start in range(0, points, LANES):
+            rows = min(LANES, points - start)
+            steps = ((sublane + start) * lane).astype(jnp.float32)
+            cosine, sine = cos_minus_sin(steps, count, inverse)
+            cosines = [cosine, cosine * turn_cos - sine * turn_sin]
+            sines = [sine, sine * turn_cos + cosine * turn_sin]
+            while len(cosines) * ROWS < rows:
+                cosines.append(twice * cosines[-1] - cosines[-2])
+                sines.append(twice * sines[-1] - sines[-2])
+            for part, values in enumerate((cosines, sines)):
+                at = pl.ds(start, rows), pl.ds(part * LANES, LANES)
+                turned_ref[i, at[0], at[1]] = jnp.concatenate(values, axis=0).astype(jnp.bfloat16)
 
 
 def least_count(pairs):
@@ -137,7 +150,7 @@
     held, fields, first,
     counts_hbm, weights_hbm, waves_hbm, stiffness_hbm, basis_hbm, grid_hbm,
     coef_ref, table_ref, choice_ref, basis_ref, wave_ref, stiffness_ref, limit_ref,
-    counts, weights, waves, levels, values, given, widened, arrived, grid_arrived,
+    counts, weights, waves, levels, values, given, widened, turned_ref, arrived, grid_arrived,
 ):
     owners, blocks = coef_ref.shape[:2]
     pairs = limit_ref.shape[0]
@@ -158,21 +171,15 @@
     for copy in (*fields_in, *small, basis_in):
         copy.start()
     least = least_count(pairs)
+    fill_turned(turned_ref, least)
     fill_tables(table_ref, width, least)
-    for copy in (*small, *fields_in, basis_in):
+    for copy in (*small, *fields_in):
         copy.wait()
     choice = slot_choice(waves, held, first, slots)
     choices = [choice] + (rest_choices(choice, held, rest) if rest else [])
     choices = [each.astype(jnp.bfloat16) for each in choices]
     for k, each in enumerate(choices):
         choice_ref[k * slots : (k + 1) * slots, :] = each
-    widened[...] = given[...].astype(jnp.float32)
-    for c in range(held):
-        for j in range(pairs):
-            strip = widened[c, pl.ds(j, owners, stride=pairs), :]
-            basis_ref[c, j * owners : (j + 1) * owners, :] = turn(strip, -first, 0).astype(
-                jnp.bfloat16
-            )
     lane = lax.broadcasted_iota(jnp.int32, (1, LANES), 1)
     padding = jnp.zeros((1, LANES - width), jnp.float32)
     own_waves = jnp.concatenate([waves[...].astype(jnp.float32), padding], axis=1)
@@ -188,49 +195,54 @@
         stiffness = stiffness + turn(own, copy * fields, 1)
     stiffness_ref[...] = stiffness
     position = lax.broadcasted_iota(jnp.int32, (1, points), 1)
-    real, imaginary, ends, scales = [], [], [], []
+    mode = lax.broadcasted_iota(jnp.int32, (1, 2 * LANES), 1) & (LANES - 1)
+    pieces = []
     for j in range(pairs):
-        count = jnp.full((1, LANES), counts[j].astype(jnp.float32))
-        limit_ref[j : j + 1, :] = count
-        ends.append(count)
-        scales.append(jnp.full((1, LANES), weights[j]) / count)
-    end_rows = lane_row(lane, ends, rows)
-    scale_rows = lane_row(lane, scales, rows)
-    for j in range(pairs):
+        limit_ref[j : j + 1, :] = jnp.full((1, LANES), counts[j].astype(jnp.float32))
         inside = jnp.where(position < counts[j], 1.0, 0.0).astype(jnp.bfloat16)
-        product = lax.dot_general(
-            table_ref[candidate_of(counts[j], j, least), :, :points],
+        product = jnp.dot(
             values[latitudes[j], :] * inside,
-            (((1,), (1,)), ((), ())),
+            turned_ref[candidate_of(counts[j], j, least)],
             preferred_element_type=jnp.float32,
         )
-        real.append(product[:width])
-        imaginary.append(product[width:])
-    mode = lax.broadcasted_iota(jnp.int32, (width, 1), 0).astype(jnp.float32)
-    tail = [jnp.zeros((width, LANES - rest), jnp.float32)] if rest else []
-    cut = [[] for _ in end_rows]
-    for pieces in (real, imaginary):
-        whole = jnp.concatenate(pieces + tail, axis=1)
-        for block, (end, scale) in enumerate(zip(end_rows, scale_rows)):
-            strip = whole[:, block * LANES : (block + 1) * LANES]
-            cut[block].append(jnp.where(2.0 * mode < end, strip * scale, 0.0))
-    cut = [jnp.concatenate(both, axis=1) for both in cut]
-    unread = jnp.zeros((LANES - width, 2 * LANES), jnp.bfloat16)
+        scale = jnp.full((1, 1), weights[j]) / jnp.full((1, 1), counts[j].astype(jnp.float32))
+        scale = jnp.where(2 * mode < counts[j], scale, 0.0)
+        pieces.append((product * scale).astype(jnp.bfloat16))
+    whole = jnp.concatenate(pieces, axis=0)
+    parts = [whole[:, part * LANES : (part + 1) * LANES] for part in range(2)]
     for block in range(blocks):
-        taken, modes = [choices[0]], [cut[block].astype(jnp.bfloat16), unread]
+        taken = [choices[0]]
+        modes = [[part[block * LANES : (block + 1) * LANES] for part in parts]]
         if rest and block == blocks - 1:
             for group, each in enumerate(choices[1:]):
-                moved = [turn(cut[-1][:, k * LANES : (k + 1) * LANES], group * rest, 1) for k in range(2)]
                 taken.append(each)
-                modes += [jnp.concatenate(moved, axis=1).astype(jnp.bfloat16), unread]
-        placed = jnp.dot(
+                above = jnp.zeros((group * rest, LANES), jnp.bfloat16)
+                below = jnp.zeros((LANES - (group + 1) * rest, LANES), jnp.bfloat16)
+                modes.append(
+                    [
+                        jnp.concatenate(
+                            [x for x in (above, part[blocks * LANES :], below) if x.shape[0]], axis=0
+                        )
+                        for part in parts
+                    ]
+                )
+        placed = lax.dot_general(
             jnp.concatenate(taken, axis=1),
-            jnp.concatenate(modes, axis=0),
+            jnp.concatenate([jnp.concatenate(both, axis=0) for both in modes], axis=1),
+            (((1,), (1,)), ((), ())),
             preferred_element_type=jnp.float32,
         )
         for part in range(2):
             strip = placed[:, part * LANES : (part + 1) * LANES]
             coef_ref[:, block, part] = strip.reshape(owners, ROWS, LANES).astype(jnp.bfloat16)
+    basis_in.wait()
+    widened[...] = given[...].astype(jnp.float32)
+    for c in range(held):
+        for j in range(pairs):
+            strip = widened[c, pl.ds(j, owners, stride=pairs), :]
+            basis_ref[c, j * owners : (j + 1) * owners, :] = turn(strip, -first, 0).astype(
+                jnp.bfloat16
+            )
 
 
 def legendre_kernel(
@@ -411,6 +423,7 @@
             pltpu.VMEM((pairs * rows, points), jnp.bfloat16),
             pltpu.VMEM(legendre.shape, jnp.bfloat16),
             pltpu.VMEM(legendre.shape, jnp.float32),
+            pltpu.VMEM((pairs + 1, points, 2 * LANES), jnp.bfloat16),
             pltpu.SemaphoreType.DMA((5,)),
             pltpu.SemaphoreType.DMA,
         ],
@@ -580,8 +593,9 @@
         width % owners == 0
         and width % (2 * ROWS) == 0
         and width <= LANES
-        and 4 * (pairs + 1) * width * points <= TABLE_BUDGET
+        and 4 * (pairs + 1) * LANES * points <= TABLE_BUDGET
         and points <= ROWS * LANES
+        and points % (2 * ROWS) == 0
         and held <= ROWS
         and lanes >= LANES
         and (rest == 0 or rest % (2 * ROWS) == 0)

time: 27.5 us -> 27.3 us (level)
  no operation moved by 1% of the time
where the time goes in v6:
time: 27.3 us; the launch traced here: 27.1 us
  blocking collectives  23.4 us (86%)
  Pallas kernels  3.68 us (13%)
    all_to_all x2, blocking collectives, exchange(): lax.all_to_all(array, 'lat', split_axis=0, concat_axis=0, axis_index_grou...  23.4 us
    pallas_call x1, Pallas kernels, on_device(): pl.pallas_call(functools.partial(analysis_kernel, held, fields, first), o...  1.7 us
    pallas_call x1, Pallas kernels, on_device(): pl.pallas_call(functools.partial(synthesis_kernel, held), out_shape=jax.S...  1.25 us
    pallas_call x1, Pallas kernels, on_device(): pl.pallas_call(functools.partial(legendre_kernel, held, fields), out_shap...  0.72 us

profile of v6, /device:TPU:0, one launch (start us, length us, event | category | flops | bytes accessed | tf_op | source)
XLA Modules:
  0.0 27.1 jit_solution(4017124661194464715)
XLA Ops:
  0.0 1.7 %analysis.1 = (bf16[16,2,2,8,128]{4,3,2,1,0:T(8,128)(2,1)S(1)}, bf16[7,192,512]{2,1,0:T(8,128)(2,1)S(1)}, bf16[640,128]{1,0:T(8,128)(2,1)S(1)}, bf16[6,96,96]{2,...) custom-call(s32[6]{0:T(128)} %counts_hbm.1, f32[6]{0:T(128)} %weights_hbm.1, ...), custom_call_target="tpu_custom_call" | custom-call | tf_op jit(solution)/shard_map/analysis/pallas_call | solution.py:405
  1.7 13.3 %all_to_all.10.recv_ref = bf16[16,2,2,8,128]{4,3,2,1,0:T(8,128)(2,1)S(1)} all-to-all(bf16[16,2,2,8,128]{4,3,2,1,0:T(8,128)(2,1)S(1)} %get-tuple-element.17), channel_id=1, replica_groups={{20,22,24,26,28,30,0,2,4,6,8,10,12,14,16,18},{21,23,25,27,29,31,1,3,5,7..., dimensions={0} | all-to-all | bytes 262144 | tf_op jit(solution)/shard_map/all_to_all | solution.py:443
  15.0 0.7 %legendre.1 = bf16[16,2,2,8,128]{4,3,2,1,0:T(8,128)(2,1)S(1)} custom-call(f32[6,128]{1,0:T(8,128)S(1)} %get-tuple-element.14.wave_ref, f32[1,128]{1,0:T(1,128)S(1)} %get-tuple-element.15.stiffness_ref, bf16[6,96,96]{2,1,0:T(8,128)(2,1)S(1)} %get-tuple-element.16.basis_ref, bf16[16,2,2,8,128]{4,3,2,1,0:T(8,128)(2,1)S(1)} %all_to_all.10.recv_ref), custom_call_target="tpu_custom_call" | custom-call | tf_op jit(solution)/shard_map/legendre/pallas_call | solution.py:447
  15.8 10.1 %all_to_all.11.recv_ref = bf16[16,2,2,8,128]{4,3,2,1,0:T(8,128)(2,1)S(1)} all-to-all(bf16[16,2,2,8,128]{4,3,2,1,0:T(8,128)(2,1)S(1)} %legendre.1), channel_id=1, replica_groups={{20,22,24,26,28,30,0,2,4,6,8,10,12,14,16,18},{21,23,25,27,29,31,1,3,5,7..., dimensions={0} | all-to-all | bytes 262144 | tf_op jit(solution)/shard_map/all_to_all | solution.py:443
  25.8 1.3 %synthesis.1 = bf16[288,400]{1,0:T(8,128)(2,1)} custom-call(f32[6,128]{1,0:T(8,128)S(1)} %get-tuple-element.12.limit_ref, bf16[640,128]{1,0:T(8,128)(2,1)S(1)} %get-tuple-element.13.choice_ref, bf16[16,2,2,8,128]{4,3,2,1,0:T(8,128)(2,1)S(1)} %all_to_all.11.recv_ref, bf16[7,192,512]{2,1,0:T(8,128)(2,1)S(1)} %get-tuple-element.18.table_ref), custom_call_target="tpu_custom_call" | custom-call | tf_op jit(solution)/shard_map/synthesis/pallas_call | solution.py:459

commit v7 on v6

--- a/solution.py
+++ b/solution.py
@@ -396,7 +396,7 @@
     blocks = pairs * rows // LANES
     rest = pairs * rows % LANES
     choices = 1 + (min(LANES // rest, held) if rest else 0)
-    first = 5 * owners // 8
+    first = 11 * owners // 16
     groups = [[(place + first) % owners for place in range(owners)]]
     vmem = pl.BlockSpec(memory_space=pltpu.VMEM)
     hbm = pl.BlockSpec(memory_space=pltpu.HBM)

time: 27.3 us -> 26.8 us (0.982)
  blocking collectives: 23.4 us -> 22.9 us
    all_to_all x2, blocking collectives: 23.4 us -> 22.9 us  [exchange(): lax.all_to_all(array, 'lat', split_axis=0, concat_axis=0, axis_index_grou...]
where the time goes in v7:
time: 26.8 us; the launch traced here: 26.6 us
  blocking collectives  22.9 us (85%)
  Pallas kernels  3.69 us (14%)
    all_to_all x2, blocking collectives, exchange(): lax.all_to_all(array, 'lat', split_axis=0, concat_axis=0, axis_index_grou...  22.9 us
    pallas_call x1, Pallas kernels, on_device(): pl.pallas_call(functools.partial(analysis_kernel, held, fields, first), o...  1.71 us
    pallas_call x1, Pallas kernels, on_device(): pl.pallas_call(functools.partial(synthesis_kernel, held), out_shape=jax.S...  1.25 us
    pallas_call x1, Pallas kernels, on_device(): pl.pallas_call(functools.partial(legendre_kernel, held, fields), out_shap...  0.72 us

profile of v7, /device:TPU:0, one launch (start us, length us, event | category | flops | bytes accessed | tf_op | source)
XLA Modules:
  0.0 26.6 jit_solution(2306557816919911000)
XLA Ops:
  0.0 1.7 %analysis.1 = (bf16[16,2,2,8,128]{4,3,2,1,0:T(8,128)(2,1)S(1)}, bf16[7,192,512]{2,1,0:T(8,128)(2,1)S(1)}, bf16[640,128]{1,0:T(8,128)(2,1)S(1)}, bf16[6,96,96]{2,...) custom-call(s32[6]{0:T(128)} %counts_hbm.1, f32[6]{0:T(128)} %weights_hbm.1, ...), custom_call_target="tpu_custom_call" | custom-call | tf_op jit(solution)/shard_map/analysis/pallas_call | solution.py:405
  1.7 12.9 %all_to_all.10.recv_ref = bf16[16,2,2,8,128]{4,3,2,1,0:T(8,128)(2,1)S(1)} all-to-all(bf16[16,2,2,8,128]{4,3,2,1,0:T(8,128)(2,1)S(1)} %get-tuple-element.17), channel_id=1, replica_groups={{22,24,26,28,30,0,2,4,6,8,10,12,14,16,18,20},{23,25,27,29,31,1,3,5,7,9,..., dimensions={0} | all-to-all | bytes 262144 | tf_op jit(solution)/shard_map/all_to_all | solution.py:443
  14.6 0.7 %legendre.1 = bf16[16,2,2,8,128]{4,3,2,1,0:T(8,128)(2,1)S(1)} custom-call(f32[6,128]{1,0:T(8,128)S(1)} %get-tuple-element.14.wave_ref, f32[1,128]{1,0:T(1,128)S(1)} %get-tuple-element.15.stiffness_ref, bf16[6,96,96]{2,1,0:T(8,128)(2,1)S(1)} %get-tuple-element.16.basis_ref, bf16[16,2,2,8,128]{4,3,2,1,0:T(8,128)(2,1)S(1)} %all_to_all.10.recv_ref), custom_call_target="tpu_custom_call" | custom-call | tf_op jit(solution)/shard_map/legendre/pallas_call | solution.py:447
  15.3 10.1 %all_to_all.11.recv_ref = bf16[16,2,2,8,128]{4,3,2,1,0:T(8,128)(2,1)S(1)} all-to-all(bf16[16,2,2,8,128]{4,3,2,1,0:T(8,128)(2,1)S(1)} %legendre.1), channel_id=1, replica_groups={{22,24,26,28,30,0,2,4,6,8,10,12,14,16,18,20},{23,25,27,29,31,1,3,5,7,9,..., dimensions={0} | all-to-all | bytes 262144 | tf_op jit(solution)/shard_map/all_to_all | solution.py:443
  25.4 1.3 %synthesis.1 = bf16[288,400]{1,0:T(8,128)(2,1)} custom-call(f32[6,128]{1,0:T(8,128)S(1)} %get-tuple-element.12.limit_ref, bf16[640,128]{1,0:T(8,128)(2,1)S(1)} %get-tuple-element.13.choice_ref, bf16[16,2,2,8,128]{4,3,2,1,0:T(8,128)(2,1)S(1)} %all_to_all.11.recv_ref, bf16[7,192,512]{2,1,0:T(8,128)(2,1)S(1)} %get-tuple-element.18.table_ref), custom_call_target="tpu_custom_call" | custom-call | tf_op jit(solution)/shard_map/synthesis/pallas_call | solution.py:459

commit v8 on v7

--- a/solution.py
+++ b/solution.py
@@ -173,14 +173,15 @@
     least = least_count(pairs)
     fill_turned(turned_ref, least)
     fill_tables(table_ref, width, least)
-    for copy in (*small, *fields_in):
-        copy.wait()
+    small[1].wait()
     choice = slot_choice(waves, held, first, slots)
     choices = [choice] + (rest_choices(choice, held, rest) if rest else [])
     choices = [each.astype(jnp.bfloat16) for each in choices]
     for k, each in enumerate(choices):
         choice_ref[k * slots : (k + 1) * slots, :] = each
     lane = lax.broadcasted_iota(jnp.int32, (1, LANES), 1)
+    for copy in (small[0], *small[2:], *fields_in):
+        copy.wait()
     padding = jnp.zeros((1, LANES - width), jnp.float32)
     own_waves = jnp.concatenate([waves[...].astype(jnp.float32), padding], axis=1)
     own_waves = pltpu.roll(own_waves, (LANES - lax.axis_index("lat") * held) % LANES, 1)
@@ -208,6 +209,14 @@
         scale = jnp.full((1, 1), weights[j]) / jnp.full((1, 1), counts[j].astype(jnp.float32))
         scale = jnp.where(2 * mode < counts[j], scale, 0.0)
         pieces.append((product * scale).astype(jnp.bfloat16))
+    basis_in.wait()
+    widened[...] = given[...].astype(jnp.float32)
+    for c in range(held):
+        for j in range(pairs):
+            strip = widened[c, pl.ds(j, owners, stride=pairs), :]
+            basis_ref[c, j * owners : (j + 1) * owners, :] = turn(strip, -first, 0).astype(
+                jnp.bfloat16
+            )
     whole = jnp.concatenate(pieces, axis=0)
     parts = [whole[:, part * LANES : (part + 1) * LANES] for part in range(2)]
     for block in range(blocks):
@@ -235,14 +244,6 @@
         for part in range(2):
             strip = placed[:, part * LANES : (part + 1) * LANES]
             coef_ref[:, block, part] = strip.reshape(owners, ROWS, LANES).astype(jnp.bfloat16)
-    basis_in.wait()
-    widened[...] = given[...].astype(jnp.float32)
-    for c in range(held):
-        for j in range(pairs):
-            strip = widened[c, pl.ds(j, owners, stride=pairs), :]
-            basis_ref[c, j * owners : (j + 1) * owners, :] = turn(strip, -first, 0).astype(
-                jnp.bfloat16
-            )
 
 
 def legendre_kernel(

time: 26.8 us -> 26.8 us (level)
  no operation moved by 1% of the time
where the time goes in v8:
time: 26.8 us; the launch traced here: 26.6 us
  blocking collectives  22.9 us (85%)
  Pallas kernels  3.69 us (14%)
    all_to_all x2, blocking collectives, exchange(): lax.all_to_all(array, 'lat', split_axis=0, concat_axis=0, axis_index_grou...  22.9 us
    pallas_call x1, Pallas kernels, on_device(): pl.pallas_call(functools.partial(analysis_kernel, held, fields, first), o...  1.72 us
    pallas_call x1, Pallas kernels, on_device(): pl.pallas_call(functools.partial(synthesis_kernel, held), out_shape=jax.S...  1.25 us
    pallas_call x1, Pallas kernels, on_device(): pl.pallas_call(functools.partial(legendre_kernel, held, fields), out_shap...  0.72 us

profile of v8, /device:TPU:0, one launch (start us, length us, event | category | flops | bytes accessed | tf_op | source)
XLA Modules:
  0.0 26.6 jit_solution(11944363676251543135)
XLA Ops:
  0.0 1.7 %analysis.1 = (bf16[16,2,2,8,128]{4,3,2,1,0:T(8,128)(2,1)S(1)}, bf16[7,192,512]{2,1,0:T(8,128)(2,1)S(1)}, bf16[640,128]{1,0:T(8,128)(2,1)S(1)}, bf16[6,96,96]{2,...) custom-call(s32[6]{0:T(128)} %counts_hbm.1, f32[6]{0:T(128)} %weights_hbm.1, ...), custom_call_target="tpu_custom_call" | custom-call | tf_op jit(solution)/shard_map/analysis/pallas_call | solution.py:406
  1.7 12.9 %all_to_all.10.recv_ref = bf16[16,2,2,8,128]{4,3,2,1,0:T(8,128)(2,1)S(1)} all-to-all(bf16[16,2,2,8,128]{4,3,2,1,0:T(8,128)(2,1)S(1)} %get-tuple-element.17), channel_id=1, replica_groups={{22,24,26,28,30,0,2,4,6,8,10,12,14,16,18,20},{23,25,27,29,31,1,3,5,7,9,..., dimensions={0} | all-to-all | bytes 262144 | tf_op jit(solution)/shard_map/all_to_all | solution.py:444
  14.6 0.7 %legendre.1 = bf16[16,2,2,8,128]{4,3,2,1,0:T(8,128)(2,1)S(1)} custom-call(f32[6,128]{1,0:T(8,128)S(1)} %get-tuple-element.14.wave_ref, f32[1,128]{1,0:T(1,128)S(1)} %get-tuple-element.15.stiffness_ref, bf16[6,96,96]{2,1,0:T(8,128)(2,1)S(1)} %get-tuple-element.16.basis_ref, bf16[16,2,2,8,128]{4,3,2,1,0:T(8,128)(2,1)S(1)} %all_to_all.10.recv_ref), custom_call_target="tpu_custom_call" | custom-call | tf_op jit(solution)/shard_map/legendre/pallas_call | solution.py:448
  15.3 10.1 %all_to_all.11.recv_ref = bf16[16,2,2,8,128]{4,3,2,1,0:T(8,128)(2,1)S(1)} all-to-all(bf16[16,2,2,8,128]{4,3,2,1,0:T(8,128)(2,1)S(1)} %legendre.1), channel_id=1, replica_groups={{22,24,26,28,30,0,2,4,6,8,10,12,14,16,18,20},{23,25,27,29,31,1,3,5,7,9,..., dimensions={0} | all-to-all | bytes 262144 | tf_op jit(solution)/shard_map/all_to_all | solution.py:444
  25.4 1.3 %synthesis.1 = bf16[288,400]{1,0:T(8,128)(2,1)} custom-call(f32[6,128]{1,0:T(8,128)S(1)} %get-tuple-element.12.limit_ref, bf16[640,128]{1,0:T(8,128)(2,1)S(1)} %get-tuple-element.13.choice_ref, bf16[16,2,2,8,128]{4,3,2,1,0:T(8,128)(2,1)S(1)} %all_to_all.11.recv_ref, bf16[7,192,512]{2,1,0:T(8,128)(2,1)S(1)} %get-tuple-element.18.table_ref), custom_call_target="tpu_custom_call" | custom-call | tf_op jit(solution)/shard_map/synthesis/pallas_call | solution.py:460

commit v9 on v8

--- a/solution.py
+++ b/solution.py
@@ -149,7 +149,7 @@
 def analysis_kernel(
     held, fields, first,
     counts_hbm, weights_hbm, waves_hbm, stiffness_hbm, basis_hbm, grid_hbm,
-    coef_ref, table_ref, choice_ref, basis_ref, wave_ref, stiffness_ref, limit_ref,
+    coef_ref, table_ref, choice_ref, basis_ref, across_ref, wave_ref, stiffness_ref, limit_ref,
     counts, weights, waves, levels, values, given, widened, turned_ref, arrived, grid_arrived,
 ):
     owners, blocks = coef_ref.shape[:2]
@@ -212,11 +212,13 @@
     basis_in.wait()
     widened[...] = given[...].astype(jnp.float32)
     for c in range(held):
+        ordered = []
         for j in range(pairs):
             strip = widened[c, pl.ds(j, owners, stride=pairs), :]
-            basis_ref[c, j * owners : (j + 1) * owners, :] = turn(strip, -first, 0).astype(
-                jnp.bfloat16
-            )
+            ordered.append(turn(strip, -first, 0))
+        ordered = jnp.concatenate(ordered, axis=0)
+        basis_ref[c] = ordered.astype(jnp.bfloat16)
+        across_ref[c] = ordered.T.astype(jnp.bfloat16)
     whole = jnp.concatenate(pieces, axis=0)
     parts = [whole[:, part * LANES : (part + 1) * LANES] for part in range(2)]
     for block in range(blocks):
@@ -247,7 +249,7 @@
 
 
 def legendre_kernel(
-    held, fields, wave_ref, stiffness_ref, basis_ref, recv_ref, send_ref, fan_in, fan_out
+    held, fields, wave_ref, stiffness_ref, basis_ref, across_ref, recv_ref, send_ref, fan_in, fan_out
 ):
     owners, blocks = recv_ref.shape[:2]
     latitudes, width = basis_ref.shape[1:]
@@ -290,11 +292,8 @@
                     here = (lane_at >= target) & (lane_at < target + size)
                     strip = jnp.where(here, turn(source, target - lane, 1), strip)
             strips.append(strip.astype(jnp.bfloat16))
-        spectra = lax.dot_general(
-            basis,
-            jnp.concatenate(strips, axis=0),
-            (((0,), (0,)), ((), ())),
-            preferred_element_type=jnp.float32,
+        spectra = jnp.dot(
+            across_ref[c], jnp.concatenate(strips, axis=0), preferred_element_type=jnp.float32
         )
         factor = 1.0 / (1.0 + stiffness_ref[...] * degree * (degree + 1.0))
         damping = jnp.where(degree < float(width), factor, 0.0)
@@ -403,19 +402,20 @@
     hbm = pl.BlockSpec(memory_space=pltpu.HBM)
     limits = pltpu.CompilerParams(vmem_limit_bytes=KERNEL_BYTES)
     exchanged = jax.ShapeDtypeStruct((owners, blocks, 2, ROWS, LANES), jnp.bfloat16)
-    coefficients, tables, choice, basis, wave_rows, levels, ends = pl.pallas_call(
+    coefficients, tables, choice, basis, across, wave_rows, levels, ends = pl.pallas_call(
         functools.partial(analysis_kernel, held, fields, first),
         out_shape=(
             exchanged,
             jax.ShapeDtypeStruct((pairs + 1, 2 * width, padded), jnp.bfloat16),
             jax.ShapeDtypeStruct((choices * slots, LANES), jnp.bfloat16),
             jax.ShapeDtypeStruct(legendre.shape, jnp.bfloat16),
+            jax.ShapeDtypeStruct((held, legendre.shape[2], legendre.shape[1]), jnp.bfloat16),
             jax.ShapeDtypeStruct((held, LANES), jnp.float32),
             jax.ShapeDtypeStruct((1, LANES), jnp.float32),
             jax.ShapeDtypeStruct((pairs, LANES), jnp.float32),
         ),
         in_specs=[hbm] * 6,
-        out_specs=(vmem,) * 7,
+        out_specs=(vmem,) * 8,
         scratch_shapes=[
             pltpu.SMEM((pairs,), jnp.int32),
             pltpu.SMEM((pairs,), jnp.float32),
@@ -448,7 +448,7 @@
     synthesised = pl.pallas_call(
         functools.partial(legendre_kernel, held, fields),
         out_shape=exchanged,
-        in_specs=[vmem] * 4,
+        in_specs=[vmem] * 5,
         out_specs=vmem,
         scratch_shapes=[
             pltpu.VMEM((blocks * 2, slots, LANES), jnp.float32),
@@ -456,7 +456,7 @@
         ],
         compiler_params=limits,
         name="legendre",
-    )(wave_rows, levels, basis, exchange(coefficients))
+    )(wave_rows, levels, basis, across, exchange(coefficients))
     result = pl.pallas_call(
         functools.partial(synthesis_kernel, held),
         out_shape=jax.ShapeDtypeStruct((pairs * rows, points), jnp.bfloat16),

time: 26.8 us -> 26.8 us (level)
  no operation moved by 1% of the time
where the time goes in v9:
time: 26.8 us; the launch traced here: 26.6 us
  blocking collectives  22.9 us (85%)
  Pallas kernels  3.62 us (14%)
    all_to_all x2, blocking collectives, exchange(): lax.all_to_all(array, 'lat', split_axis=0, concat_axis=0, axis_index_grou...  22.9 us
    pallas_call x1, Pallas kernels, on_device(): pl.pallas_call(functools.partial(analysis_kernel, held, fields, first), o...  1.7 us
    pallas_call x1, Pallas kernels, on_device(): pl.pallas_call(functools.partial(synthesis_kernel, held), out_shape=jax.S...  1.25 us
    pallas_call x1, Pallas kernels, on_device(): pl.pallas_call(functools.partial(legendre_kernel, held, fields), out_shap...  0.67 us

profile of v9, /device:TPU:0, one launch (start us, length us, event | category | flops | bytes accessed | tf_op | source)
XLA Modules:
  0.0 26.6 jit_solution(5234901734747748934)
XLA Ops:
  0.0 1.7 %analysis.1 = (bf16[16,2,2,8,128]{4,3,2,1,0:T(8,128)(2,1)S(1)}, bf16[7,192,512]{2,1,0:T(8,128)(2,1)S(1)}, bf16[640,128]{1,0:T(8,128)(2,1)S(1)}, bf16[6,96,96]{2,...) custom-call(s32[6]{0:T(128)} %counts_hbm.1, ...), custom_call_target="tpu_custom_call" | custom-call | tf_op jit(solution)/shard_map/analysis/pallas_call | solution.py:405
  1.7 12.9 %all_to_all.10.recv_ref = bf16[16,2,2,8,128]{4,3,2,1,0:T(8,128)(2,1)S(1)} all-to-all(bf16[16,2,2,8,128]{4,3,2,1,0:T(8,128)(2,1)S(1)} %get-tuple-element.19), channel_id=1, replica_groups={{22,24,26,28,30,0,2,4,6,8,10,12,14,16,18,20},{23,25,27,29,31,1,3,5,7,9,..., dimensions={0} | all-to-all | bytes 262144 | tf_op jit(solution)/shard_map/all_to_all | solution.py:444
  14.6 0.7 %legendre.1 = bf16[16,2,2,8,128]{4,3,2,1,0:T(8,128)(2,1)S(1)} custom-call(f32[6,128]{1,0:T(8,128)S(1)} %get-tuple-element.15.wave_ref, f32[1,128]{1,0:T(1,128)S(1)} %get-tuple-element.16.stiffness_ref, bf16[6,96,96]{2,1,0:T(8,128)(2,1)S(1)} %get-tuple-element.17.basis_ref, bf16[6,96,96]{2,1,0:T(8,128)(2,1)S(1)} %get-tuple-element.18.across_ref, ...), custom_call_target="tpu_custom_call" | custom-call | tf_op jit(solution)/shard_map/legendre/pallas_call | solution.py:448
  15.3 10.1 %all_to_all.11.recv_ref = bf16[16,2,2,8,128]{4,3,2,1,0:T(8,128)(2,1)S(1)} all-to-all(bf16[16,2,2,8,128]{4,3,2,1,0:T(8,128)(2,1)S(1)} %legendre.1), channel_id=1, replica_groups={{22,24,26,28,30,0,2,4,6,8,10,12,14,16,18,20},{23,25,27,29,31,1,3,5,7,9,..., dimensions={0} | all-to-all | bytes 262144 | tf_op jit(solution)/shard_map/all_to_all | solution.py:444
  25.3 1.3 %synthesis.1 = bf16[288,400]{1,0:T(8,128)(2,1)} custom-call(f32[6,128]{1,0:T(8,128)S(1)} %get-tuple-element.13.limit_ref, bf16[640,128]{1,0:T(8,128)(2,1)S(1)} %get-tuple-element.14.choice_ref, bf16[16,2,2,8,128]{4,3,2,1,0:T(8,128)(2,1)S(1)} %all_to_all.11.recv_ref, bf16[7,192,512]{2,1,0:T(8,128)(2,1)S(1)} %get-tuple-element.20.table_ref), custom_call_target="tpu_custom_call" | custom-call | tf_op jit(solution)/shard_map/synthesis/pallas_call | solution.py:460

commit v10 on v9

--- a/solution.py
+++ b/solution.py
@@ -149,7 +149,7 @@
 def analysis_kernel(
     held, fields, first,
     counts_hbm, weights_hbm, waves_hbm, stiffness_hbm, basis_hbm, grid_hbm,
-    coef_ref, table_ref, choice_ref, basis_ref, across_ref, wave_ref, stiffness_ref, limit_ref,
+    coef_ref, table_ref, choice_ref, basis_ref, across_ref, wave_ref, damping_ref, limit_ref,
     counts, weights, waves, levels, values, given, widened, turned_ref, arrived, grid_arrived,
 ):
     owners, blocks = coef_ref.shape[:2]
@@ -194,7 +194,11 @@
     stiffness = own
     for copy in range(1, 4):
         stiffness = stiffness + turn(own, copy * fields, 1)
-    stiffness_ref[...] = stiffness
+    degree_step = lax.broadcasted_iota(jnp.int32, (width, 1), 0).astype(jnp.float32)
+    for c in range(held):
+        degree = degree_step + own_waves[:, c : c + 1]
+        factor = 1.0 / (1.0 + stiffness * degree * (degree + 1.0))
+        damping_ref[c] = jnp.where(degree < float(width), factor, 0.0)
     position = lax.broadcasted_iota(jnp.int32, (1, points), 1)
     mode = lax.broadcasted_iota(jnp.int32, (1, 2 * LANES), 1) & (LANES - 1)
     pieces = []
@@ -249,7 +253,7 @@
 
 
 def legendre_kernel(
-    held, fields, wave_ref, stiffness_ref, basis_ref, across_ref, recv_ref, send_ref, fan_in, fan_out
+    held, fields, wave_ref, damping_ref, basis_ref, across_ref, recv_ref, send_ref, fan_in, fan_out
 ):
     owners, blocks = recv_ref.shape[:2]
     latitudes, width = basis_ref.shape[1:]
@@ -274,12 +278,10 @@
     south = ((lane_at >= fields) & (lane_at < 2 * fields)) | (lane_at >= 3 * fields)
     offset = lax.broadcasted_iota(jnp.int32, (width, 1), 0)
     parity = jnp.where((offset & 1) == 0, 1.0, -1.0)
-    offset = offset.astype(jnp.float32)
     empty = jnp.zeros((owners, LANES), jnp.float32)
     folded = {}
     for c in range(held):
         wave = wave_ref[c : c + 1, :]
-        degree = offset + wave
         basis = basis_ref[c]
         strips = []
         for j in range(pairs):
@@ -295,10 +297,8 @@
         spectra = jnp.dot(
             across_ref[c], jnp.concatenate(strips, axis=0), preferred_element_type=jnp.float32
         )
-        factor = 1.0 / (1.0 + stiffness_ref[...] * degree * (degree + 1.0))
-        damping = jnp.where(degree < float(width), factor, 0.0)
         other = jnp.where(south, turn(spectra, fields, 1), turn(spectra, -fields, 1))
-        scaled = ((spectra + parity * other) * damping).astype(jnp.bfloat16)
+        scaled = ((spectra + parity * other) * damping_ref[c]).astype(jnp.bfloat16)
         returned = jnp.dot(basis, scaled, preferred_element_type=jnp.float32)
         returned = returned * jnp.where(wave == 0.0, 1.0, 2.0)
         for part in range(2):
@@ -402,7 +402,7 @@
     hbm = pl.BlockSpec(memory_space=pltpu.HBM)
     limits = pltpu.CompilerParams(vmem_limit_bytes=KERNEL_BYTES)
     exchanged = jax.ShapeDtypeStruct((owners, blocks, 2, ROWS, LANES), jnp.bfloat16)
-    coefficients, tables, choice, basis, across, wave_rows, levels, ends = pl.pallas_call(
+    coefficients, tables, choice, basis, across, wave_rows, damping, ends = pl.pallas_call(
         functools.partial(analysis_kernel, held, fields, first),
         out_shape=(
             exchanged,
@@ -411,7 +411,7 @@
             jax.ShapeDtypeStruct(legendre.shape, jnp.bfloat16),
             jax.ShapeDtypeStruct((held, legendre.shape[2], legendre.shape[1]), jnp.bfloat16),
             jax.ShapeDtypeStruct((held, LANES), jnp.float32),
-            jax.ShapeDtypeStruct((1, LANES), jnp.float32),
+            jax.ShapeDtypeStruct((held, width, LANES), jnp.float32),
             jax.ShapeDtypeStruct((pairs, LANES), jnp.float32),
         ),
         in_specs=[hbm] * 6,
@@ -456,7 +456,7 @@
         ],
         compiler_params=limits,
         name="legendre",
-    )(wave_rows, levels, basis, across, exchange(coefficients))
+    )(wave_rows, damping, basis, across, exchange(coefficients))
     result = pl.pallas_call(
         functools.partial(synthesis_kernel, held),
         out_shape=jax.ShapeDtypeStruct((pairs * rows, points), jnp.bfloat16),

time: 26.8 us -> 26.9 us (level)
  no operation moved by 1% of the time
where the time goes in v10:
time: 26.9 us; the launch traced here: 26.7 us
  blocking collectives  22.9 us (85%)
  Pallas kernels  3.72 us (14%)
    all_to_all x2, blocking collectives, exchange(): lax.all_to_all(array, 'lat', split_axis=0, concat_axis=0, axis_index_grou...  22.9 us
    pallas_call x1, Pallas kernels, on_device(): pl.pallas_call(functools.partial(analysis_kernel, held, fields, first), o...  1.79 us
    pallas_call x1, Pallas kernels, on_device(): pl.pallas_call(functools.partial(synthesis_kernel, held), out_shape=jax.S...  1.25 us
    pallas_call x1, Pallas kernels, on_device(): pl.pallas_call(functools.partial(legendre_kernel, held, fields), out_shap...  0.67 us

profile of v10, /device:TPU:0, one launch (start us, length us, event | category | flops | bytes accessed | tf_op | source)
XLA Modules:
  0.0 26.7 jit_solution(4671372226974546995)
XLA Ops:
  0.0 1.8 %analysis.1 = (bf16[16,2,2,8,128]{4,3,2,1,0:T(8,128)(2,1)S(1)}, bf16[7,192,512]{2,1,0:T(8,128)(2,1)S(1)}, bf16[640,128]{1,0:T(8,128)(2,1)S(1)}, bf16[6,96,96]{2,...) custom-call(s32[6]{0:T(128)} %counts_hbm.1, ...), custom_call_target="tpu_custom_call" | custom-call | tf_op jit(solution)/shard_map/analysis/pallas_call | solution.py:405
  1.8 12.9 %all_to_all.10.recv_ref = bf16[16,2,2,8,128]{4,3,2,1,0:T(8,128)(2,1)S(1)} all-to-all(bf16[16,2,2,8,128]{4,3,2,1,0:T(8,128)(2,1)S(1)} %get-tuple-element.19), channel_id=1, replica_groups={{22,24,26,28,30,0,2,4,6,8,10,12,14,16,18,20},{23,25,27,29,31,1,3,5,7,9,..., dimensions={0} | all-to-all | bytes 262144 | tf_op jit(solution)/shard_map/all_to_all | solution.py:444
  14.7 0.7 %legendre.1 = bf16[16,2,2,8,128]{4,3,2,1,0:T(8,128)(2,1)S(1)} custom-call(f32[6,128]{1,0:T(8,128)S(1)} %get-tuple-element.15.wave_ref, f32[6,96,128]{2,1,0:T(8,128)S(1)} %get-tuple-element.16.damping_ref, bf16[6,96,96]{2,1,0:T(8,128)(2,1)S(1)} %get-tuple-element.17.basis_ref, bf16[6,96,96]{2,1,0:T(8,128)(2,1)S(1)} %get-tuple-element.18.across_ref, ...), custom_call_target="tpu_custom_call" | custom-call | tf_op jit(solution)/shard_map/legendre/pallas_call | solution.py:448
  15.4 10.1 %all_to_all.11.recv_ref = bf16[16,2,2,8,128]{4,3,2,1,0:T(8,128)(2,1)S(1)} all-to-all(bf16[16,2,2,8,128]{4,3,2,1,0:T(8,128)(2,1)S(1)} %legendre.1), channel_id=1, replica_groups={{22,24,26,28,30,0,2,4,6,8,10,12,14,16,18,20},{23,25,27,29,31,1,3,5,7,9,..., dimensions={0} | all-to-all | bytes 262144 | tf_op jit(solution)/shard_map/all_to_all | solution.py:444
  25.4 1.2 %synthesis.1 = bf16[288,400]{1,0:T(8,128)(2,1)} custom-call(f32[6,128]{1,0:T(8,128)S(1)} %get-tuple-element.13.limit_ref, bf16[640,128]{1,0:T(8,128)(2,1)S(1)} %get-tuple-element.14.choice_ref, bf16[16,2,2,8,128]{4,3,2,1,0:T(8,128)(2,1)S(1)} %all_to_all.11.recv_ref, bf16[7,192,512]{2,1,0:T(8,128)(2,1)S(1)} %get-tuple-element.20.table_ref), custom_call_target="tpu_custom_call" | custom-call | tf_op jit(solution)/shard_map/synthesis/pallas_call | solution.py:460
